TPU v7x, 128 devices: a whole 4x4x4 slice. The times are simulated.
128 devices in a mesh: section: 4 (over z), mp: 32 (over y, x, core).
Axes of the slice: x: 4, y: 4, z: 4, core: 2. Of those that a mesh axis runs over, the one named last changes fastest.
Arguments:
- entering_hidden: bfloat16 [4, 256, 8192], P('section', None, 'mp'), may hold values from -12 to 12
- section_weight: bfloat16 [4, 8192, 8192], P('section', None, 'mp'), may hold values from -0.0625 to 0.0625
- section_norm_gain: bfloat16 [4, 8192], P('section', 'mp'), may hold values from 0.5 to 1.5
- plugin_narrowing_factors: bfloat16 [4, 32, 8192, 64], P('section', 'mp'), may hold values from -0.0625 to 0.0625
- plugin_widening_factors: bfloat16 [4, 32, 64, 8192], P('section', 'mp'), may hold values from -0.75 to 0.75
- reward_head: bfloat16 [8192], P('mp'), may hold values from -0.0625 to 0.0625
- adapter_of_block: int32 [4, 2], replicated, may hold values from 0 to 31
- live_block_rows: int32 [4, 2], P('section'), may hold values from 1 to 128
Outputs:
- hidden_out: bfloat16 [4, 256, 8192], P('section', None, 'mp')
- scores: float32 [4, 256], P('section')
All inputs are finite; a program needn't handle non-finite values.
Results may differ from a plain program's by a relative error of at most 0.022.
Values may be sent and summed in bfloat16 or wider, within the bound.
A program may use at most 64 MiB of HBM per device.

v0:
```python
import jax
import jax.numpy as jnp
from jax import lax
from jax.sharding import PartitionSpec as P

BLOCK = 128


def shifted(value, axis, steps):
    count = lax.axis_size(axis)
    initial, last = (max(0, -steps), min(count, count - steps))
    return lax.ppermute(value, axis, [(source, source + steps) for source in range(initial, last)])


def shards(
    entering_hidden,
    section_weight,
    section_norm_gain,
    plugin_narrowing_factors,
    plugin_widening_factors,
    reward_head,
    adapter_of_block,
    live_block_rows,
):
    sections = lax.axis_size("section")
    section_index = lax.axis_index("section")
    owners = lax.axis_size("mp")
    owner_index = lax.axis_index("mp")
    batches_here, rows, piece_extent = entering_hidden.shape
    micro = batches_here * sections
    width = piece_extent * owners
    blocks = rows // BLOCK
    owned_blocks = plugin_narrowing_factors.shape[1]
    adapters = owned_blocks * owners
    rank_position = plugin_narrowing_factors.shape[3]
    weight = section_weight[0]
    gain = section_norm_gain[0].astype(jnp.float32)
    fed = lax.all_gather(entering_hidden, "section", axis=0, tiled=True)
    up_map_columns = lax.all_to_all(
        plugin_widening_factors, "mp", split_axis=3, concat_axis=1, tiled=True
    )[0]
    up_table = up_map_columns.reshape(adapters, rank_position * piece_extent)

    def layer_of_section(hidden_state, adapter_numbers):
        hidden_f = hidden_state.astype(jnp.float32)
        onehot = (
            adapter_numbers[:, None] == jnp.arange(adapters, dtype=jnp.int32)[None, :]
        ).astype(jnp.bfloat16)
        squares = lax.psum(jnp.sum(hidden_f * hidden_f, axis=1), "mp")
        rescaled_activation = (
            hidden_f * lax.rsqrt(squares / width + 1e-05)[:, None] * gain[None, :]
        ).astype(jnp.bfloat16)
        gathered = lax.all_gather(rescaled_activation, "mp", axis=1, tiled=True)
        base = jnp.dot(gathered, weight, preferred_element_type=jnp.float32)
        local_ids = adapter_numbers - owner_index * owned_blocks
        mine = (local_ids >= 0) & (local_ids < owned_blocks)
        products = []
        for block_number in range(blocks):
            segment = gathered[block_number * BLOCK : (block_number + 1) * BLOCK]
            picked = jnp.clip(local_ids[block_number], 0, owned_blocks - 1)
            products.append(
                lax.cond(
                    mine[block_number],
                    lambda incoming_rows, selected_adapter: jnp.dot(
                        incoming_rows,
                        plugin_narrowing_factors[0, selected_adapter],
                        preferred_element_type=jnp.float32,
                    ),
                    lambda incoming_rows, selected_adapter: jnp.zeros(
                        (BLOCK, rank_position), jnp.float32
                    ),
                    segment,
                    picked,
                )
            )
        compressed_projection = jnp.stack(products)
        compressed_projection = lax.psum(compressed_projection.astype(jnp.bfloat16), "mp")
        chosen_expansion_matrix = (
            jnp.dot(onehot, up_table, preferred_element_type=jnp.float32)
            .astype(jnp.bfloat16)
            .reshape(blocks, rank_position, piece_extent)
        )
        thin_correction = jnp.einsum(
            "sin,sny->siy",
            compressed_projection,
            chosen_expansion_matrix,
            preferred_element_type=jnp.float32,
        ).reshape(rows, piece_extent)
        return (hidden_f + base + 2.0 * thin_correction).astype(jnp.bfloat16)

    def tick(step, carry):
        moving, finished = carry
        arrived = shifted(moving, "section", 1)
        feed_now = lax.dynamic_index_in_dim(fed, jnp.minimum(step, micro - 1), 0, keepdims=False)
        current_signal = jnp.where(section_index == 0, feed_now, arrived)
        selected_adapter = step - section_index
        valid = (selected_adapter >= 0) & (selected_adapter < micro)
        position = jnp.clip(selected_adapter, 0, micro - 1)
        adapter_numbers = lax.dynamic_index_in_dim(adapter_of_block, position, 0, keepdims=False)
        output = layer_of_section(current_signal, adapter_numbers)
        entry_tuple = valid & (section_index == sections - 1)
        previous = lax.dynamic_index_in_dim(finished, position, 0, keepdims=False)
        finished = lax.dynamic_update_index_in_dim(
            finished, jnp.where(entry_tuple, output, previous), position, 0
        )
        return (output, finished)

    start_moving = jnp.zeros((rows, piece_extent), jnp.bfloat16)
    start_finished = jnp.zeros((micro, rows, piece_extent), jnp.bfloat16)
    moving, finished = lax.fori_loop(0, micro + sections - 1, tick, (start_moving, start_finished))
    hidden_out = lax.psum_scatter(
        finished.astype(jnp.float32).astype(jnp.bfloat16),
        "section",
        scatter_dimension=0,
        tiled=True,
    )
    partial_score = jnp.sum(
        hidden_out.astype(jnp.float32) * reward_head.astype(jnp.float32)[None, None, :], axis=2
    )
    raw = lax.psum(partial_score, "mp")
    place = jnp.arange(rows, dtype=jnp.int32) % BLOCK
    limits = jnp.repeat(live_block_rows, BLOCK, axis=1)
    scores = jnp.where(place[None, :] < limits, raw, jnp.float32(0.0))
    return (hidden_out, scores)


def solution(mesh):
    placed = (
        P("section", None, "mp"),
        P("section", None, "mp"),
        P("section", "mp"),
        P("section", "mp", None, None),
        P("section", "mp", None, None),
        P("mp"),
        P(),
        P("section", None),
    )
    return jax.shard_map(
        shards,
        mesh=mesh,
        in_specs=placed,
        out_specs=(P("section", None, "mp"), P("section", None)),
        check_vma=False,
    )
```

profile of v0, /device:TPU:97, one launch (start us, length us, event | category | flops | bytes accessed | tf_op | source)
XLA Modules:
  0.0 1949.0 jit_solution(13879705828689722286)
XLA Ops:
  8.0 9.2 copy.21
  17.7 45.2 %reduce.1 = bf16[8192,64]{1,0:T(8,128)(2,1)S(1)} reduce(bf16[8192,1,1,64]{3,2,1,0:T(2,128)(2,1)} %bitcast.80, bf16[]{:T(256)} %broadcast.105), dimensions={1,2}, to_apply=%bitcast.49.reduce_sub_computation | reduce | bytes 2097154
  62.9 2.2 reshape.80
  65.2 7.8 all-to-all-start
  73.0 2.0 copy.25
  75.1 11.5 all_gather.11
  86.6 3.4 all-to-all-done
  90.0 7.0 reshape.81
  97.0 8.2 copy.22
  106.4 1746.6 %while.17 = (s32[]{:T(128)}, bf16[256,256]{1,0:T(8,128)(2,1)}, bf16[4,256,256]{2,1,0:T(8,128)(2,1)}, pred[]{:T(512)}, bf16[4,256,256]{2,1,0:T(8,128)(2,1)}, /*in...) while((s32[]{:T(128)}, bf16[256,256]{1,0:T(8,128)(2,1)}, ...), condition=%wide.region_8.9_spmd.clone, body=%wide.region_0.8_spmd.clone.sunk | while | flops 1353712128 | bytes 31792572 | solution.py:110
  107.7 5.2 collective-permute-done
  114.0 63.3 %psum.36 = f32[256]{0:T(256)S(1)} all-reduce(f32[256]{0:T(256)S(1)} %get-tuple-element.499), channel_id=1, replica_groups=mesh['section'=4,'mp'=32] {'mp'}, use_global_device_ids=true, to_apply=%region_2.2 | all-reduce | flops 256 | bytes 2048 | tf_op jit(solution)/shard_map/while/body/eval_jaxpr/psum | solution.py:49
  181.1 42.4 %all-gather.2.cloned.1.call-done = bf16[256,8192]{1,0:T(8,128)(2,1)} async-done(((bf16[256,256]{1,0:T(8,128)(2,1)}), bf16[256,8192]{1,0:T(8,128)(2,1)}) %all-gather.2.cloned.1.call-update) | async-done | bytes 4194320 | tf_op jit(solution)/shard_map/while/body/eval_jaxpr/all_gather | solution.py:53
  223.5 121.1 %psum.37 = bf16[2,128,64]{1,2,0:T(8,128)(2,1)S(1)} all-reduce(bf16[2,128,64]{1,2,0:T(8,128)(2,1)S(1)} %pad_maximum_fusion.2), channel_id=1, replica_groups=mesh['section'=4,'mp'=32] {'mp'}, use_global_device_ids=true, to_apply=%region_7.7 | all-reduce | flops 16384 | bytes 65536 | tf_op jit(solution)/shard_map/while/body/eval_jaxpr/psum | solution.py:77
  344.8 5.4 bitcast_dynamic-update-slice_fusion.2
  351.2 1.3 collective-permute-start
  352.5 4.4 collective-permute-done
  357.9 68.8 %psum.36 = f32[256]{0:T(256)S(1)} all-reduce(f32[256]{0:T(256)S(1)} %get-tuple-element.499), channel_id=1, replica_groups=mesh['section'=4,'mp'=32] {'mp'}, use_global_device_ids=true, to_apply=%region_2.2 | all-reduce | flops 256 | bytes 2048 | tf_op jit(solution)/shard_map/while/body/eval_jaxpr/psum | solution.py:49
  430.6 42.4 %all-gather.2.cloned.1.call-done = bf16[256,8192]{1,0:T(8,128)(2,1)} async-done(((bf16[256,256]{1,0:T(8,128)(2,1)}), bf16[256,8192]{1,0:T(8,128)(2,1)}) %all-gather.2.cloned.1.call-update) | async-done | bytes 4194320 | tf_op jit(solution)/shard_map/while/body/eval_jaxpr/all_gather | solution.py:53
  473.0 121.1 %psum.37 = bf16[2,128,64]{1,2,0:T(8,128)(2,1)S(1)} all-reduce(bf16[2,128,64]{1,2,0:T(8,128)(2,1)S(1)} %pad_maximum_fusion.2), channel_id=1, replica_groups=mesh['section'=4,'mp'=32] {'mp'}, use_global_device_ids=true, to_apply=%region_7.7 | all-reduce | flops 16384 | bytes 65536 | tf_op jit(solution)/shard_map/while/body/eval_jaxpr/psum | solution.py:77
  594.3 5.4 bitcast_dynamic-update-slice_fusion.2
  601.9 4.4 collective-permute-done
  607.4 68.8 %psum.36 = f32[256]{0:T(256)S(1)} all-reduce(f32[256]{0:T(256)S(1)} %get-tuple-element.499), channel_id=1, replica_groups=mesh['section'=4,'mp'=32] {'mp'}, use_global_device_ids=true, to_apply=%region_2.2 | all-reduce | flops 256 | bytes 2048 | tf_op jit(solution)/shard_map/while/body/eval_jaxpr/psum | solution.py:49
  680.0 42.4 %all-gather.2.cloned.1.call-done = bf16[256,8192]{1,0:T(8,128)(2,1)} async-done(((bf16[256,256]{1,0:T(8,128)(2,1)}), bf16[256,8192]{1,0:T(8,128)(2,1)}) %all-gather.2.cloned.1.call-update) | async-done | bytes 4194320 | tf_op jit(solution)/shard_map/while/body/eval_jaxpr/all_gather | solution.py:53
  722.4 121.1 %psum.37 = bf16[2,128,64]{1,2,0:T(8,128)(2,1)S(1)} all-reduce(bf16[2,128,64]{1,2,0:T(8,128)(2,1)S(1)} %pad_maximum_fusion.2), channel_id=1, replica_groups=mesh['section'=4,'mp'=32] {'mp'}, use_global_device_ids=true, to_apply=%region_7.7 | all-reduce | flops 16384 | bytes 65536 | tf_op jit(solution)/shard_map/while/body/eval_jaxpr/psum | solution.py:77
  843.7 5.4 bitcast_dynamic-update-slice_fusion.2
  851.4 4.4 collective-permute-done
  856.8 68.8 %psum.36 = f32[256]{0:T(256)S(1)} all-reduce(f32[256]{0:T(256)S(1)} %get-tuple-element.499), channel_id=1, replica_groups=mesh['section'=4,'mp'=32] {'mp'}, use_global_device_ids=true, to_apply=%region_2.2 | all-reduce | flops 256 | bytes 2048 | tf_op jit(solution)/shard_map/while/body/eval_jaxpr/psum | solution.py:49
  929.5 43.4 %all-gather.2.cloned.1.call-done = bf16[256,8192]{1,0:T(8,128)(2,1)} async-done(((bf16[256,256]{1,0:T(8,128)(2,1)}), bf16[256,8192]{1,0:T(8,128)(2,1)}) %all-gather.2.cloned.1.call-update) | async-done | bytes 4194320 | tf_op jit(solution)/shard_map/while/body/eval_jaxpr/all_gather | solution.py:53
  972.9 121.1 %psum.37 = bf16[2,128,64]{1,2,0:T(8,128)(2,1)S(1)} all-reduce(bf16[2,128,64]{1,2,0:T(8,128)(2,1)S(1)} %pad_maximum_fusion.2), channel_id=1, replica_groups=mesh['section'=4,'mp'=32] {'mp'}, use_global_device_ids=true, to_apply=%region_7.7 | all-reduce | flops 16384 | bytes 65536 | tf_op jit(solution)/shard_map/while/body/eval_jaxpr/psum | solution.py:77
  1094.2 5.4 bitcast_dynamic-update-slice_fusion.2
  1101.9 6.0 collective-permute-done
  1108.9 68.5 %psum.36 = f32[256]{0:T(256)S(1)} all-reduce(f32[256]{0:T(256)S(1)} %get-tuple-element.499), channel_id=1, replica_groups=mesh['section'=4,'mp'=32] {'mp'}, use_global_device_ids=true, to_apply=%region_2.2 | all-reduce | flops 256 | bytes 2048 | tf_op jit(solution)/shard_map/while/body/eval_jaxpr/psum | solution.py:49
  1181.3 43.6 %all-gather.2.cloned.1.call-done = bf16[256,8192]{1,0:T(8,128)(2,1)} async-done(((bf16[256,256]{1,0:T(8,128)(2,1)}), bf16[256,8192]{1,0:T(8,128)(2,1)}) %all-gather.2.cloned.1.call-update) | async-done | bytes 4194320 | tf_op jit(solution)/shard_map/while/body/eval_jaxpr/all_gather | solution.py:53
  1225.0 123.7 %psum.37 = bf16[2,128,64]{1,2,0:T(8,128)(2,1)S(1)} all-reduce(bf16[2,128,64]{1,2,0:T(8,128)(2,1)S(1)} %pad_maximum_fusion.2), channel_id=1, replica_groups=mesh['section'=4,'mp'=32] {'mp'}, use_global_device_ids=true, to_apply=%region_7.7 | all-reduce | flops 16384 | bytes 65536 | tf_op jit(solution)/shard_map/while/body/eval_jaxpr/psum | solution.py:77
  1348.9 5.4 bitcast_dynamic-update-slice_fusion.2
  1356.5 4.4 collective-permute-done
  1361.9 68.8 %psum.36 = f32[256]{0:T(256)S(1)} all-reduce(f32[256]{0:T(256)S(1)} %get-tuple-element.499), channel_id=1, replica_groups=mesh['section'=4,'mp'=32] {'mp'}, use_global_device_ids=true, to_apply=%region_2.2 | all-reduce | flops 256 | bytes 2048 | tf_op jit(solution)/shard_map/while/body/eval_jaxpr/psum | solution.py:49
  1434.6 42.2 %all-gather.2.cloned.1.call-done = bf16[256,8192]{1,0:T(8,128)(2,1)} async-done(((bf16[256,256]{1,0:T(8,128)(2,1)}), bf16[256,8192]{1,0:T(8,128)(2,1)}) %all-gather.2.cloned.1.call-update) | async-done | bytes 4194320 | tf_op jit(solution)/shard_map/while/body/eval_jaxpr/all_gather | solution.py:53
  1476.8 121.1 %psum.37 = bf16[2,128,64]{1,2,0:T(8,128)(2,1)S(1)} all-reduce(bf16[2,128,64]{1,2,0:T(8,128)(2,1)S(1)} %pad_maximum_fusion.2), channel_id=1, replica_groups=mesh['section'=4,'mp'=32] {'mp'}, use_global_device_ids=true, to_apply=%region_7.7 | all-reduce | flops 16384 | bytes 65536 | tf_op jit(solution)/shard_map/while/body/eval_jaxpr/psum | solution.py:77
  1598.1 5.4 bitcast_dynamic-update-slice_fusion.2
  1605.7 4.4 collective-permute-done
  1611.2 68.8 %psum.36 = f32[256]{0:T(256)S(1)} all-reduce(f32[256]{0:T(256)S(1)} %get-tuple-element.499), channel_id=1, replica_groups=mesh['section'=4,'mp'=32] {'mp'}, use_global_device_ids=true, to_apply=%region_2.2 | all-reduce | flops 256 | bytes 2048 | tf_op jit(solution)/shard_map/while/body/eval_jaxpr/psum | solution.py:49
  1683.8 42.3 %all-gather.2.cloned.1.call-done = bf16[256,8192]{1,0:T(8,128)(2,1)} async-done(((bf16[256,256]{1,0:T(8,128)(2,1)}), bf16[256,8192]{1,0:T(8,128)(2,1)}) %all-gather.2.cloned.1.call-update) | async-done | bytes 4194320 | tf_op jit(solution)/shard_map/while/body/eval_jaxpr/all_gather | solution.py:53
  1726.2 121.1 %psum.37 = bf16[2,128,64]{1,2,0:T(8,128)(2,1)S(1)} all-reduce(bf16[2,128,64]{1,2,0:T(8,128)(2,1)S(1)} %pad_maximum_fusion.2), channel_id=1, replica_groups=mesh['section'=4,'mp'=32] {'mp'}, use_global_device_ids=true, to_apply=%region_7.7 | all-reduce | flops 16384 | bytes 65536 | tf_op jit(solution)/shard_map/while/body/eval_jaxpr/psum | solution.py:77
  1847.5 5.4 bitcast_dynamic-update-slice_fusion.2
  1853.5 22.0 %reduce-scatter.2.cloned.1.call-done = bf16[1,256,256]{2,1,0:T(8,128)(2,1)} async-done(((bf16[4,256,256]{2,1,0:T(8,128)(2,1)}), bf16[1,256,256]{2,1,0:T(8,128)(2,1)}) %reduce-scatter.2.cloned.1.call-update) | async-done | bytes 131088 | tf_op jit(solution)/shard_map/reduce_scatter | solution.py:111
  1876.6 64.3 %psum.31 = f32[1,256]{1,0:T(1,128)S(1)} all-reduce(f32[1,256]{1,0:T(1,128)S(1)} %bitcast.87), channel_id=1, replica_groups=mesh['section'=4,'mp'=32] {'mp'}, use_global_device_ids=true, to_apply=%region_11.12 | all-reduce | flops 256 | bytes 2048 | tf_op jit(solution)/shard_map/psum | solution.py:120
  (141 shorter events, 44.7 us)
Async XLA Ops:
  62.9 12.1 copy-start.1
  62.9 12.2 copy-start.2
  62.9 12.2 copy-start
  65.2 24.8 %all-to-all-start = ((bf16[32,2,8192]{2,1,0:T(2,128)(2,1)}), bf16[32,2,8192]{2,1,0:T(2,128)(2,1)S(1)}, u32[]{:S(2)}, u32[]{:S(2)}) async-start(bf16[32,2,8192]{2,1,0:T(2,128)(2,1)} %reshape.80), calls=%async_computation | async-start | bytes 2097152 | tf_op jit(solution)/shard_map/all_to_all | solution.py:39
  106.3 1747.1 %copy-start.3 = (bf16[256]{0:T(256)(128)(2,1)S(1)}, bf16[256]{0:T(256)(128)(2,1)}, u32[]{:S(2)}) copy-start(bf16[256]{0:T(256)(128)(2,1)} %param.19) | copy-start | bytes 1540
  106.4 1834.6 %copy-start.4 = (s32[1,2]{1,0:T(1,128)S(1)}, s32[1,2]{1,0:T(1,128)}, u32[]{:S(2)}) copy-start(s32[1,2]{1,0:T(1,128)} %param.21) | copy-start | bytes 28
  106.4 117.2 %all-gather.2.cloned.1.call-start = ((), (), s32[]{:S(2)}) async-start(), calls=%async_computation.3 | async-start | bytes 4325376 | tf_op jit(solution)/shard_map/while/body/eval_jaxpr/all_gather | solution.py:53
  106.4 6.5 collective-permute-start
  350.3 122.7 %all-gather.2.cloned.1.call-start = ((), (), s32[]{:S(2)}) async-start(), calls=%async_computation.3 | async-start | bytes 4325376 | tf_op jit(solution)/shard_map/while/body/eval_jaxpr/all_gather | solution.py:53
  351.2 5.7 collective-permute-start
  599.7 122.7 %all-gather.2.cloned.1.call-start = ((), (), s32[]{:S(2)}) async-start(), calls=%async_computation.3 | async-start | bytes 4325376 | tf_op jit(solution)/shard_map/while/body/eval_jaxpr/all_gather | solution.py:53
  600.6 5.7 collective-permute-start
  849.1 123.7 %all-gather.2.cloned.1.call-start = ((), (), s32[]{:S(2)}) async-start(), calls=%async_computation.3 | async-start | bytes 4325376 | tf_op jit(solution)/shard_map/while/body/eval_jaxpr/all_gather | solution.py:53
  850.1 5.7 collective-permute-start
  1099.6 125.3 %all-gather.2.cloned.1.call-start = ((), (), s32[]{:S(2)}) async-start(), calls=%async_computation.3 | async-start | bytes 4325376 | tf_op jit(solution)/shard_map/while/body/eval_jaxpr/all_gather | solution.py:53
  1100.6 7.3 collective-permute-start
  1354.3 122.5 %all-gather.2.cloned.1.call-start = ((), (), s32[]{:S(2)}) async-start(), calls=%async_computation.3 | async-start | bytes 4325376 | tf_op jit(solution)/shard_map/while/body/eval_jaxpr/all_gather | solution.py:53
  1355.2 5.7 collective-permute-start
  1603.5 122.7 %all-gather.2.cloned.1.call-start = ((), (), s32[]{:S(2)}) async-start(), calls=%async_computation.3 | async-start | bytes 4325376 | tf_op jit(solution)/shard_map/while/body/eval_jaxpr/all_gather | solution.py:53
  1604.4 5.7 collective-permute-start
  1852.9 22.6 %reduce-scatter.2.cloned.1.call-start = ((), (), s32[]{:S(2)}) async-start(), calls=%async_computation.2 | async-start | bytes 655360 | tf_op jit(solution)/shard_map/reduce_scatter | solution.py:111
Sparse Core Ops, SparseCore 0:
  178.2 45.2 all-gather.1
  427.7 45.2 all-gather.1
  677.1 45.2 all-gather.1
  926.5 46.2 all-gather.1
  1178.4 46.4 all-gather.1
  1431.7 45.0 all-gather.1
  1680.9 45.2 all-gather.1
Sparse Core Ops, SparseCore 1:
  1856.3 19.1 reduce-scatter.1
where the time goes:
time: 1960 us; the launch traced here: 1950 us
  blocking collectives  1400 us (71%)
  waiting for transfers between devices  358 us (18%)
  other arithmetic  65.1 us (3%)
  matrix products  41.8 us (2%)
  local copies, waits for them, and re-layouts  41.1 us (2%)
    psum x7, blocking collectives, layer_of_section(): lax.psum(compressed_projection.astype(jnp.bfloat16), 'mp')  850 us
    psum x7, blocking collectives, layer_of_section(): squares = lax.psum(jnp.sum(hidden_f * hidden_f, axis=1), 'mp')  476 us
    all_gather x7, waiting for transfers between devices, layer_of_section(): gathered = lax.all_gather(rescaled_activation, 'mp', axis=1, tiled=True)  299 us
    psum x1, blocking collectives, shards(): raw = lax.psum(partial_score, 'mp')  64.3 us
    unnamed x2, other arithmetic  45.2 us
  transfers between devices with their start and end apart: 16, of which 16 were waited for; matrix products, arithmetic and copies ran while one was open for 1% of the time, Pallas kernels for 0%

commit v1 on v0

v1 whole, which is shorter than its diff:
```python
import functools

import jax
import jax.numpy as jnp
from jax import lax
from jax.experimental import pallas as pl
from jax.experimental.pallas import tpu as pltpu
from jax.sharding import PartitionSpec as P

MESH = pl.DeviceIdType.MESH
BLOCK = 128
CHUNK = 64
COLOURS = 4
STEPS = 4
PIECE = CHUNK // COLOURS
RING = 4
WIDTH = 256
RANK = 64
LANES = 128

A, B, C, D = (1, 0), (3, 0), (0, 1), (0, 3)
ORDER = ((A, B, C, D), (B, A, D, C), (C, D, A, B), (D, C, B, A))


def flipped(position, mask):
    if mask == 0:
        return position
    if mask == 1:
        return position + 1 - 2 * lax.rem(position, 2)
    if mask == 2:
        return lax.rem(position + 2, 4)
    return 3 - position


def slots():
    tables = []
    for order in ORDER:
        table = {}
        for slot in range(2**STEPS):
            bits_x, bits_y = 0, 0
            for step in range(STEPS):
                if slot >> step & 1:
                    bits_x ^= order[step][0]
                    bits_y ^= order[step][1]
            table[bits_y * 4 + bits_x] = slot
        tables.append(table)
    return tables


SLOT = slots()


def encode(value, lane):
    high = value.astype(jnp.bfloat16).astype(jnp.float32)
    low = pltpu.roll(value - high, 1, axis=1)
    return jnp.where(lane == RANK + 1, low, value).astype(jnp.bfloat16)


def decode(message, lane):
    value = message.astype(jnp.float32)
    low = pltpu.roll(value, LANES - 1, axis=1)
    value = jnp.where(lane == RANK, value + low, value)
    return jnp.where(lane == RANK + 1, 0.0, value)


def kernel(
    chunks,
    adapter_ref,
    live_ref,
    enter_ref,
    weight_ref,
    gain_ref,
    narrow_ref,
    widen_ref,
    head_ref,
    out_ref,
    score_ref,
    hz,
    gathered,
    sums_out,
    sums_in,
    running,
    final_sums,
    sib_sums,
    part_out,
    part_in,
    own_part,
    next_h,
    w_own,
    w_sib,
    narrow_v,
    packed,
    narrow_t,
    widen_t,
    finished,
    score_part,
    score_all,
    gs,
    gr,
    as_,
    ar_,
    xs,
    xr,
    zs,
    zr,
    fs,
    fr,
    once,
):
    section = lax.axis_index("section")
    mp = lax.axis_index("mp")
    core = lax.rem(mp, 2)
    chip = lax.div(mp, 2)
    x = lax.rem(chip, RING)
    y = lax.div(chip, RING)
    other = mp + 1 - 2 * core
    per_micro = 256 // CHUNK

    def mesh_id(where, rank):
        return {"section": where, "mp": rank}

    barrier = pltpu.get_barrier_semaphore()
    for offset in range(1, 32):
        pl.semaphore_signal(
            barrier, inc=1, device_id=mesh_id(section, lax.rem(mp + offset, 32)), device_id_type=MESH
        )
    for offset in range(1, 4):
        pl.semaphore_signal(
            barrier, inc=1, device_id=mesh_id(lax.rem(section + offset, 4), mp), device_id_type=MESH
        )

    narrow_load = pltpu.make_async_copy(narrow_ref, narrow_v, once.at[0])
    narrow_load.start()

    def chip_of(rel):
        return flipped(y, rel // 4) * RING + flipped(x, rel % 4)

    for rel in range(16):
        rows = pl.ds(pl.multiple_of((chip_of(rel) * 2 + core) * WIDTH, WIDTH), WIDTH)
        pltpu.make_async_copy(
            weight_ref.at[rows], w_own.at[pl.ds(rel * WIDTH, WIDTH)], once.at[1]
        ).start()

    @pl.when(section == 0)
    def _():
        for part in range(per_micro):
            pltpu.make_async_copy(
                enter_ref.at[pl.ds(part * CHUNK, CHUNK)], hz.at[part], zr.at[part]
            ).start()

    pl.semaphore_wait(barrier, 34)

    @pl.when(section > 0)
    def _():
        for part in range(per_micro):
            index = section * per_micro + part
            pltpu.make_async_remote_copy(
                src_ref=enter_ref.at[pl.ds(part * CHUNK, CHUNK)],
                dst_ref=hz.at[index],
                send_sem=fs.at[part],
                recv_sem=zr.at[index],
                device_id=mesh_id(0, mp),
                device_id_type=MESH,
            ).start()

    def swap_weight(rel):
        rows = pl.ds(pl.multiple_of((chip_of(rel) * 2 + 1 - core) * WIDTH, WIDTH), WIDTH)
        return pltpu.make_async_remote_copy(
            src_ref=weight_ref.at[rows],
            dst_ref=w_sib.at[pl.ds(rel * WIDTH, WIDTH)],
            send_sem=once.at[2],
            recv_sem=once.at[3],
            device_id=mesh_id(section, other),
            device_id_type=MESH,
        )

    for rel in range(16):
        swap_weight(rel).start()

    def widen_send(offset):
        target = lax.rem(mp + offset, 32)
        return pltpu.make_async_remote_copy(
            src_ref=widen_ref.at[:, pl.ds(pl.multiple_of(target * WIDTH, WIDTH), WIDTH)],
            dst_ref=widen_t.at[mp],
            send_sem=once.at[4],
            recv_sem=once.at[5],
            device_id=mesh_id(section, target),
            device_id_type=MESH,
        )

    def narrow_send(offset):
        target = lax.rem(mp + offset, 32)
        return pltpu.make_async_remote_copy(
            src_ref=packed.at[target],
            dst_ref=narrow_t.at[mp],
            send_sem=once.at[6],
            recv_sem=once.at[7],
            device_id=mesh_id(section, target),
            device_id_type=MESH,
        )

    narrow_load.wait()

    @pl.loop(0, 32)
    def _(target):
        tile = narrow_v[pl.ds(pl.multiple_of(target * WIDTH, WIDTH), WIDTH), :]
        packed[target] = jnp.concatenate([tile[:128], tile[128:]], axis=1)

    @pl.loop(1, 32)
    def _(offset):
        narrow_send(offset).start()
        widen_send(offset).start()

    pltpu.make_async_copy(packed.at[mp], narrow_t.at[mp], once.at[7]).start()
    pltpu.make_async_copy(
        widen_ref.at[:, pl.ds(pl.multiple_of(mp * WIDTH, WIDTH), WIDTH)], widen_t.at[mp], once.at[5]
    ).start()

    lane = lax.broadcasted_iota(jnp.int32, (CHUNK, LANES), 1)
    gain = gain_ref[...].astype(jnp.float32)

    def adapter_of(index):
        return adapter_ref[lax.div(index, per_micro), lax.div(lax.rem(index, per_micro), BLOCK // CHUNK)]

    def step_copies(index, step):
        ring_slot = lax.rem(index, 4)
        copies = []
        for colour in range(COLOURS):
            mask_x, mask_y = ORDER[colour][step]
            partner = (flipped(y, mask_y) * RING + flipped(x, mask_x)) * 2 + core
            count = 2**step
            copies.append(
                pltpu.make_async_remote_copy(
                    src_ref=gathered.at[index, colour, pl.ds(0, count)],
                    dst_ref=gathered.at[index, colour, pl.ds(count, count)],
                    send_sem=gs.at[ring_slot, step, colour],
                    recv_sem=gr.at[ring_slot, step, colour],
                    device_id=mesh_id(section, partner),
                    device_id_type=MESH,
                )
            )
            rows = pl.ds(colour * PIECE, PIECE)
            copies.append(
                pltpu.make_async_remote_copy(
                    src_ref=sums_out.at[index, step, rows],
                    dst_ref=sums_in.at[index, step, rows],
                    send_sem=as_.at[ring_slot, step, colour],
                    recv_sem=ar_.at[ring_slot, step, colour],
                    device_id=mesh_id(section, partner),
                    device_id_type=MESH,
                )
            )
        return copies

    def start_step(index, step):
        for copy in step_copies(index, step):
            copy.start()

    def finish_step(index, step):
        for copy in step_copies(index, step):
            copy.wait()
        total = running[index] + decode(sums_in[index, step], lane)
        if step < STEPS - 1:
            running[index] = total
            sums_out[index, step + 1] = encode(total, lane)
        else:
            final_sums[index] = total

    def prepare(index):
        pltpu.make_async_copy(hz.at[index], hz.at[index], zr.at[index]).wait()
        h = hz[index].astype(jnp.float32)
        squares = jnp.sum(h * h, axis=1, keepdims=True)
        scaled = (h * gain).astype(jnp.bfloat16)
        for colour in range(COLOURS):
            gathered[index, colour, 0] = scaled[colour * PIECE : (colour + 1) * PIECE]
        maps = narrow_t[adapter_of(index)]
        first = jnp.dot(scaled[:, :128], maps, preferred_element_type=jnp.float32)
        second = jnp.dot(scaled[:, 128:], maps, preferred_element_type=jnp.float32)
        inner = first + pltpu.roll(second, RANK, axis=1)
        value = jnp.where(lane < RANK, inner, jnp.where(lane == RANK, squares, 0.0))
        running[index] = value
        sums_out[index, 0] = encode(value, lane)
        start_step(index, 0)

    def left_side(index):
        return jnp.concatenate(
            [
                jnp.concatenate([gathered[index, colour, SLOT[colour][rel]] for colour in range(COLOURS)], axis=0)
                for rel in range(16)
            ],
            axis=1,
        )

    def swaps(index):
        ring_slot = lax.rem(index, 4)
        sums = pltpu.make_async_remote_copy(
            src_ref=final_sums.at[index],
            dst_ref=sib_sums.at[index],
            send_sem=xs.at[ring_slot, 0],
            recv_sem=xr.at[ring_slot, 0],
            device_id=mesh_id(section, other),
            device_id_type=MESH,
        )
        parts = pltpu.make_async_remote_copy(
            src_ref=part_out.at[index],
            dst_ref=part_in.at[index],
            send_sem=xs.at[ring_slot, 1],
            recv_sem=xr.at[ring_slot, 1],
            device_id=mesh_id(section, other),
            device_id_type=MESH,
        )
        return sums, parts

    def multiply_sibling(index):
        sums, parts = swaps(index)
        sums.start()
        part_out[index] = jnp.dot(left_side(index), w_sib[...], preferred_element_type=jnp.float32)
        parts.start()

    def multiply_own(index):
        own_part[...] = jnp.dot(left_side(index), w_own[...], preferred_element_type=jnp.float32)

    def onward(index):
        return pltpu.make_async_remote_copy(
            src_ref=next_h.at[index],
            dst_ref=hz.at[index],
            send_sem=zs.at[index],
            recv_sem=zr.at[index],
            device_id=mesh_id(lax.rem(section + 1, 4), mp),
            device_id_type=MESH,
        )

    def homeward(index):
        home = lax.div(index, per_micro)
        part = lax.rem(index, per_micro)
        return pltpu.make_async_remote_copy(
            src_ref=next_h.at[index],
            dst_ref=finished.at[part],
            send_sem=zs.at[index],
            recv_sem=fr.at[part],
            device_id=mesh_id(home, mp),
            device_id_type=MESH,
        )

    def combine(index):
        sums, parts = swaps(index)
        sums.wait()
        parts.wait()
        total = final_sums[index] + sib_sums[index]
        squares = jnp.sum(jnp.where(lane == RANK, total, 0.0), axis=1, keepdims=True)
        scale = lax.rsqrt(squares / (WIDTH * 32) + 1e-05)
        inner = total[:, :RANK].astype(jnp.bfloat16)
        delta = jnp.dot(inner, widen_t[adapter_of(index)], preferred_element_type=jnp.float32)
        base = own_part[...] + part_in[index]
        h = hz[index].astype(jnp.float32)
        next_h[index] = (h + scale * (base + 2.0 * delta)).astype(jnp.bfloat16)

        @pl.when(section < 3)
        def _():
            onward(index).start()

        @pl.when(section == 3)
        def _():
            @pl.when(index < 3 * per_micro)
            def _():
                homeward(index).start()

            @pl.when(index >= 3 * per_micro)
            def _():
                part = lax.rem(index, per_micro)
                pltpu.make_async_copy(next_h.at[index], finished.at[part], fr.at[part]).start()

    pltpu.make_async_copy(narrow_t, narrow_t, once.at[7]).wait()
    pltpu.make_async_copy(widen_t, widen_t, once.at[5]).wait()
    pltpu.make_async_copy(w_own, w_own, once.at[1]).wait()
    pltpu.make_async_copy(w_sib, w_sib, once.at[3]).wait()
    pltpu.make_async_copy(w_sib, w_sib, once.at[2]).wait()
    pltpu.make_async_copy(narrow_t.at[pl.ds(0, 31)], narrow_t.at[pl.ds(0, 31)], once.at[6]).wait()
    pltpu.make_async_copy(widen_t.at[pl.ds(0, 31)], widen_t.at[pl.ds(0, 31)], once.at[4]).wait()

    @pl.loop(0, chunks + 2)
    def _(tick):
        @pl.when((tick >= 1) & (tick <= chunks))
        def _():
            finish_step(tick - 1, 2)
            start_step(tick - 1, 3)

        @pl.when(tick < chunks)
        def _():
            prepare(tick)

        @pl.when(tick >= 2)
        def _():
            finish_step(tick - 2, 3)
            multiply_sibling(tick - 2)

        @pl.when(tick < chunks)
        def _():
            finish_step(tick, 0)
            start_step(tick, 1)

        @pl.when(tick >= 2)
        def _():
            multiply_own(tick - 2)
            combine(tick - 2)

        @pl.when(tick < chunks)
        def _():
            finish_step(tick, 1)
            start_step(tick, 2)

    @pl.when(section > 0)
    def _():
        for part in range(per_micro):
            pltpu.make_async_copy(hz.at[0], hz.at[0], fs.at[part]).wait()

    @pl.loop(0, chunks)
    def _(index):
        @pl.when((section < 3) | (index < 3 * per_micro))
        def _():
            pltpu.make_async_copy(next_h.at[index], next_h.at[index], zs.at[index]).wait()

    for part in range(per_micro):
        pltpu.make_async_copy(finished.at[part], finished.at[part], fr.at[part]).wait()
    hidden = jnp.concatenate([finished[part] for part in range(per_micro)], axis=0)
    out_ref[...] = hidden
    head = jnp.broadcast_to(head_ref[...], (8, WIDTH))
    partial = lax.dot_general(head, hidden, (((1,), (1,)), ((), ())), preferred_element_type=jnp.float32)
    score_part[...] = partial[:1]

    def score_send(offset):
        return pltpu.make_async_remote_copy(
            src_ref=score_part,
            dst_ref=score_all.at[mp],
            send_sem=once.at[8],
            recv_sem=once.at[9],
            device_id=mesh_id(section, lax.rem(mp + offset, 32)),
            device_id_type=MESH,
        )

    @pl.loop(1, 32)
    def _(offset):
        score_send(offset).start()

    pltpu.make_async_copy(score_part, score_all.at[mp], once.at[9]).start()
    pltpu.make_async_copy(score_all, score_all, once.at[9]).wait()
    pltpu.make_async_copy(score_all.at[pl.ds(0, 31)], score_all.at[pl.ds(0, 31)], once.at[8]).wait()
    raw = jnp.sum(score_all[...], axis=0)
    place = lax.broadcasted_iota(jnp.int32, (1, 2 * BLOCK), 1)
    limit = jnp.where(place < BLOCK, live_ref[0, 0], live_ref[0, 1])
    score_ref[...] = jnp.where(lax.rem(place, BLOCK) < limit, raw, 0.0)


def shards(
    entering_hidden,
    section_weight,
    section_norm_gain,
    plugin_narrowing_factors,
    plugin_widening_factors,
    reward_head,
    adapter_of_block,
    live_block_rows,
):
    chunks = 1024 // CHUNK
    bf16, f32 = jnp.bfloat16, jnp.float32
    vmem = pl.BlockSpec(memory_space=pltpu.VMEM)
    smem = pl.BlockSpec(memory_space=pltpu.SMEM)
    anywhere = pl.BlockSpec(memory_space=pl.ANY)
    dma = pltpu.SemaphoreType.DMA
    hidden, scores = pl.pallas_call(
        functools.partial(kernel, chunks),
        out_shape=(
            jax.ShapeDtypeStruct((256, WIDTH), bf16),
            jax.ShapeDtypeStruct((1, 256), f32),
        ),
        in_specs=[smem, smem, anywhere, anywhere, vmem, anywhere, anywhere, vmem],
        out_specs=(vmem, vmem),
        scratch_shapes=[
            pltpu.VMEM((chunks, CHUNK, WIDTH), bf16),
            pltpu.VMEM((chunks, COLOURS, 16, PIECE, WIDTH), bf16),
            pltpu.VMEM((chunks, STEPS, CHUNK, LANES), bf16),
            pltpu.VMEM((chunks, STEPS, CHUNK, LANES), bf16),
            pltpu.VMEM((chunks, CHUNK, LANES), f32),
            pltpu.VMEM((chunks, CHUNK, LANES), f32),
            pltpu.VMEM((chunks, CHUNK, LANES), f32),
            pltpu.VMEM((chunks, CHUNK, WIDTH), f32),
            pltpu.VMEM((chunks, CHUNK, WIDTH), f32),
            pltpu.VMEM((CHUNK, WIDTH), f32),
            pltpu.VMEM((chunks, CHUNK, WIDTH), bf16),
            pltpu.VMEM((16 * WIDTH, WIDTH), bf16),
            pltpu.VMEM((16 * WIDTH, WIDTH), bf16),
            pltpu.VMEM((32 * WIDTH, RANK), bf16),
            pltpu.VMEM((32, 128, LANES), bf16),
            pltpu.VMEM((32, 128, LANES), bf16),
            pltpu.VMEM((32, RANK, WIDTH), bf16),
            pltpu.VMEM((256 // CHUNK, CHUNK, WIDTH), bf16),
            pltpu.VMEM((1, 256), f32),
            pltpu.VMEM((32, 1, 256), f32),
            dma((4, STEPS, COLOURS)),
            dma((4, STEPS, COLOURS)),
            dma((4, STEPS, COLOURS)),
            dma((4, STEPS, COLOURS)),
            dma((4, 2)),
            dma((4, 2)),
            dma((chunks,)),
            dma((chunks,)),
            dma((4,)),
            dma((4,)),
            dma((10,)),
        ],
        compiler_params=pltpu.CompilerParams(
            collective_id=0, has_side_effects=True, vmem_limit_bytes=60 * 1024 * 1024
        ),
    )(
        adapter_of_block,
        live_block_rows,
        entering_hidden[0],
        section_weight[0],
        section_norm_gain,
        plugin_narrowing_factors[0, 0],
        plugin_widening_factors[0, 0],
        reward_head[None, :],
    )
    return hidden[None], scores


def solution(mesh):
    placed = (
        P("section", None, "mp"),
        P("section", None, "mp"),
        P("section", "mp"),
        P("section", "mp", None, None),
        P("section", "mp", None, None),
        P("mp"),
        P(),
        P("section", None),
    )
    return jax.shard_map(
        shards,
        mesh=mesh,
        in_specs=placed,
        out_specs=(P("section", None, "mp"), P("section", None)),
        check_vma=False,
    )
```

time: 1960 us -> 338 us (0.17)
  blocking collectives: 1400 us -> 0 us
  waiting for transfers between devices: 358 us -> 0 us
  Pallas kernels: 0 us -> 329 us
  other arithmetic: 65.1 us -> 0 us
  matrix products: 41.8 us -> 0 us
  local copies, waits for them, and re-layouts: 41.1 us -> 8.13 us
    psum x15 -> x0, blocking collectives: 1390 us -> none  [the longest x7 850 us: layer_of_section(): lax.psum(compressed_projection.astype(jnp.bfloat16), 'mp')]
    pallas_call x0 -> x1, Pallas kernels: none -> 329 us  [shards(): pl.pallas_call(functools.partial(kernel, chunks), out_shape=(jax.ShapeDty...]
    all_gather x7 -> x0, waiting for transfers between devices: 299 us -> none  [layer_of_section(): gathered = lax.all_gather(rescaled_activation, 'mp', axis=1, tiled=True)]
    unnamed x2 -> x0, other arithmetic: 45.2 us -> none
    dot_general x21 -> x0, matrix products: 41.8 us -> none  [the longest x7 38 us: layer_of_section(): base = jnp.dot(gathered, weight, preferred_element_type=jnp.float32)]
    ppermute x7 -> x0, waiting for transfers between devices: 33.3 us -> none  [shifted(): lax.ppermute(value, axis, [(source, source + steps) for source in range(i...]
    reduce_scatter x1 -> x0, waiting for transfers between devices: 22 us -> none  [shards(): lax.psum_scatter(finished.astype(jnp.float32).astype(jnp.bfloat16), 'sect...]
  transfers between devices with their start and end apart: 16 -> 0, of which waited for: 16 -> 0; matrix products, arithmetic and copies ran while one was open for 1% -> 0% of each run, Pallas kernels for 0% -> 0%
where the time goes in v1:
time: 338 us
  Pallas kernels  329 us (97%)
  local copies, waits for them, and re-layouts  8.13 us (2%)
    pallas_call x1, Pallas kernels, shards(): pl.pallas_call(functools.partial(kernel, chunks), out_shape=(jax.ShapeDty...  329 us
    unnamed x4, local copies, waits for them, and re-layouts  6.91 us

profile of v1, /device:TPU:97, one launch (start us, length us, event | category | flops | bytes accessed | tf_op | source)
XLA Modules:
  0.0 337.8 jit_solution(14567972690278277694)
XLA Ops:
  0.6 1.2 broadcast_in_dim.6.head_ref
  1.9 1.3 copy.11.adapter_ref
  3.2 2.8 copy.10
  6.0 329.1 %shard_map.95 = (bf16[256,256]{1,0:T(8,128)(2,1)}, f32[1,256]{1,0:T(1,128)}) custom-call(s32[4,2]{1,0:T(4,128)} %copy.11.adapter_ref, s32[1,2]{1,0:T(1,128)} %live_ref.1, bf16[256,256]{1,0:T(8,128)(2,1)} %bitcast.8, bf16[8192,256]{1,0:T(8,128)(2,1)} %bitcast.6, bf16[1,256]{1,0:T(2,128)(2,1)} %gain_ref.1, bf16[8192,64]{1,0:T(8,128)(2,1)} %bitcast.5, ...), custom_call_target="tpu_custom_call" | custom-call | tf_op jit(solution)/shard_map/pallas_call | solution.py:470
  335.0 1.6 copy.14
  336.6 1.2 copy.15

commit v2 on v1

--- a/solution.py
+++ b/solution.py
@@ -10,16 +10,16 @@
 MESH = pl.DeviceIdType.MESH
 BLOCK = 128
 CHUNK = 64
-COLOURS = 4
-STEPS = 4
+COLOURS = 2
+PHASES = 2
 PIECE = CHUNK // COLOURS
 RING = 4
 WIDTH = 256
 RANK = 64
 LANES = 128
-
-A, B, C, D = (1, 0), (3, 0), (0, 1), (0, 3)
-ORDER = ((A, B, C, D), (B, A, D, C), (C, D, A, B), (D, C, B, A))
+RETIRE = 3
+
+FAR = ((2, 2), (3, 2), (2, 3), (1, 2), (2, 1), (0, 2), (2, 0), (3, 1), (1, 3), (3, 3), (1, 1), (0, 3), (3, 0), (0, 1), (1, 0))
 
 
 def flipped(position, mask):
@@ -32,22 +32,8 @@
     return 3 - position
 
 
-def slots():
-    tables = []
-    for order in ORDER:
-        table = {}
-        for slot in range(2**STEPS):
-            bits_x, bits_y = 0, 0
-            for step in range(STEPS):
-                if slot >> step & 1:
-                    bits_x ^= order[step][0]
-                    bits_y ^= order[step][1]
-            table[bits_y * 4 + bits_x] = slot
-        tables.append(table)
-    return tables
-
-
-SLOT = slots()
+def slot_of(colour, rel):
+    return (rel // 4, rel % 4) if colour == 0 else (rel % 4, rel // 4)
 
 
 def encode(value, lane):
@@ -88,8 +74,6 @@
     next_h,
     w_own,
     w_sib,
-    narrow_v,
-    packed,
     narrow_t,
     widen_t,
     finished,
@@ -129,9 +113,6 @@
             barrier, inc=1, device_id=mesh_id(lax.rem(section + offset, 4), mp), device_id_type=MESH
         )
 
-    narrow_load = pltpu.make_async_copy(narrow_ref, narrow_v, once.at[0])
-    narrow_load.start()
-
     def chip_of(rel):
         return flipped(y, rel // 4) * RING + flipped(x, rel % 4)
 
@@ -174,47 +155,27 @@
             device_id_type=MESH,
         )
 
+    def columns(rank):
+        return pl.ds(pl.multiple_of(rank * WIDTH, WIDTH), WIDTH)
+
+    def spread(source, table, send, receive):
+        for other_core in (0, 1):
+            for mask_x, mask_y in FAR + (((0, 0),) if other_core else ()):
+                rank = (flipped(y, mask_y) * RING + flipped(x, mask_x)) * 2 + (1 - core if other_core else core)
+                pltpu.make_async_remote_copy(
+                    src_ref=source.at[:, columns(rank)],
+                    dst_ref=table.at[mp],
+                    send_sem=once.at[send],
+                    recv_sem=once.at[receive],
+                    device_id=mesh_id(section, rank),
+                    device_id_type=MESH,
+                ).start()
+        pltpu.make_async_copy(source.at[:, columns(mp)], table.at[mp], once.at[receive]).start()
+
+    spread(narrow_ref, narrow_t, 6, 7)
     for rel in range(16):
         swap_weight(rel).start()
-
-    def widen_send(offset):
-        target = lax.rem(mp + offset, 32)
-        return pltpu.make_async_remote_copy(
-            src_ref=widen_ref.at[:, pl.ds(pl.multiple_of(target * WIDTH, WIDTH), WIDTH)],
-            dst_ref=widen_t.at[mp],
-            send_sem=once.at[4],
-            recv_sem=once.at[5],
-            device_id=mesh_id(section, target),
-            device_id_type=MESH,
-        )
-
-    def narrow_send(offset):
-        target = lax.rem(mp + offset, 32)
-        return pltpu.make_async_remote_copy(
-            src_ref=packed.at[target],
-            dst_ref=narrow_t.at[mp],
-            send_sem=once.at[6],
-            recv_sem=once.at[7],
-            device_id=mesh_id(section, target),
-            device_id_type=MESH,
-        )
-
-    narrow_load.wait()
-
-    @pl.loop(0, 32)
-    def _(target):
-        tile = narrow_v[pl.ds(pl.multiple_of(target * WIDTH, WIDTH), WIDTH), :]
-        packed[target] = jnp.concatenate([tile[:128], tile[128:]], axis=1)
-
-    @pl.loop(1, 32)
-    def _(offset):
-        narrow_send(offset).start()
-        widen_send(offset).start()
-
-    pltpu.make_async_copy(packed.at[mp], narrow_t.at[mp], once.at[7]).start()
-    pltpu.make_async_copy(
-        widen_ref.at[:, pl.ds(pl.multiple_of(mp * WIDTH, WIDTH), WIDTH)], widen_t.at[mp], once.at[5]
-    ).start()
+    spread(widen_ref, widen_t, 4, 5)
 
     lane = lax.broadcasted_iota(jnp.int32, (CHUNK, LANES), 1)
     gain = gain_ref[...].astype(jnp.float32)
@@ -222,47 +183,50 @@
     def adapter_of(index):
         return adapter_ref[lax.div(index, per_micro), lax.div(lax.rem(index, per_micro), BLOCK // CHUNK)]
 
-    def step_copies(index, step):
+    def phase_copies(index, phase):
         ring_slot = lax.rem(index, 4)
         copies = []
-        for colour in range(COLOURS):
-            mask_x, mask_y = ORDER[colour][step]
-            partner = (flipped(y, mask_y) * RING + flipped(x, mask_x)) * 2 + core
-            count = 2**step
-            copies.append(
-                pltpu.make_async_remote_copy(
-                    src_ref=gathered.at[index, colour, pl.ds(0, count)],
-                    dst_ref=gathered.at[index, colour, pl.ds(count, count)],
-                    send_sem=gs.at[ring_slot, step, colour],
-                    recv_sem=gr.at[ring_slot, step, colour],
-                    device_id=mesh_id(section, partner),
-                    device_id_type=MESH,
+        for mask in (2, 3, 1):
+            for colour in range(COLOURS):
+                mask_x, mask_y = (mask, 0) if colour == phase else (0, mask)
+                partner = (flipped(y, mask_y) * RING + flipped(x, mask_x)) * 2 + core
+                piece = gathered.at[index, colour]
+                rows = pl.ds(colour * PIECE, PIECE)
+                copies.append(
+                    pltpu.make_async_remote_copy(
+                        src_ref=piece.at[0, 0] if phase == 0 else piece.at[0],
+                        dst_ref=piece.at[0, mask] if phase == 0 else piece.at[mask],
+                        send_sem=gs.at[ring_slot, phase, colour, mask - 1],
+                        recv_sem=gr.at[ring_slot, phase, colour, mask - 1],
+                        device_id=mesh_id(section, partner),
+                        device_id_type=MESH,
+                    )
                 )
-            )
-            rows = pl.ds(colour * PIECE, PIECE)
-            copies.append(
-                pltpu.make_async_remote_copy(
-                    src_ref=sums_out.at[index, step, rows],
-                    dst_ref=sums_in.at[index, step, rows],
-                    send_sem=as_.at[ring_slot, step, colour],
-                    recv_sem=ar_.at[ring_slot, step, colour],
-                    device_id=mesh_id(section, partner),
-                    device_id_type=MESH,
+                copies.append(
+                    pltpu.make_async_remote_copy(
+                        src_ref=sums_out.at[index, phase, rows],
+                        dst_ref=sums_in.at[index, phase, mask - 1, rows],
+                        send_sem=as_.at[ring_slot, phase, colour, mask - 1],
+                        recv_sem=ar_.at[ring_slot, phase, colour, mask - 1],
+                        device_id=mesh_id(section, partner),
+                        device_id_type=MESH,
+                    )
                 )
-            )
         return copies
 
-    def start_step(index, step):
-        for copy in step_copies(index, step):
+    def start_phase(index, phase):
+        for copy in phase_copies(index, phase):
             copy.start()
 
-    def finish_step(index, step):
-        for copy in step_copies(index, step):
-            copy.wait()
-        total = running[index] + decode(sums_in[index, step], lane)
-        if step < STEPS - 1:
+    def finish_phase(index, phase):
+        for copy in phase_copies(index, phase):
+            copy.wait_recv()
+        total = running[index]
+        for peer in range(3):
+            total = total + decode(sums_in[index, phase, peer], lane)
+        if phase == 0:
             running[index] = total
-            sums_out[index, step + 1] = encode(total, lane)
+            sums_out[index, 1] = encode(total, lane)
         else:
             final_sums[index] = total
 
@@ -272,20 +236,20 @@
         squares = jnp.sum(h * h, axis=1, keepdims=True)
         scaled = (h * gain).astype(jnp.bfloat16)
         for colour in range(COLOURS):
-            gathered[index, colour, 0] = scaled[colour * PIECE : (colour + 1) * PIECE]
-        maps = narrow_t[adapter_of(index)]
-        first = jnp.dot(scaled[:, :128], maps, preferred_element_type=jnp.float32)
-        second = jnp.dot(scaled[:, 128:], maps, preferred_element_type=jnp.float32)
-        inner = first + pltpu.roll(second, RANK, axis=1)
-        value = jnp.where(lane < RANK, inner, jnp.where(lane == RANK, squares, 0.0))
+            gathered[index, colour, 0, 0] = scaled[colour * PIECE : (colour + 1) * PIECE]
+        inner = lax.dot_general(
+            scaled, narrow_t[adapter_of(index)], (((1,), (1,)), ((), ())), preferred_element_type=jnp.float32
+        )
+        half_lane = lax.broadcasted_iota(jnp.int32, (CHUNK, LANES - RANK), 1)
+        value = jnp.concatenate([inner, jnp.where(half_lane == 0, squares, 0.0)], axis=1)
         running[index] = value
         sums_out[index, 0] = encode(value, lane)
-        start_step(index, 0)
+        start_phase(index, 0)
 
     def left_side(index):
         return jnp.concatenate(
             [
-                jnp.concatenate([gathered[index, colour, SLOT[colour][rel]] for colour in range(COLOURS)], axis=0)
+                jnp.concatenate([gathered[(index, colour) + slot_of(colour, rel)] for colour in range(COLOURS)], axis=0)
                 for rel in range(16)
             ],
             axis=1,
@@ -344,8 +308,8 @@
 
     def combine(index):
         sums, parts = swaps(index)
-        sums.wait()
-        parts.wait()
+        sums.wait_recv()
+        parts.wait_recv()
         total = final_sums[index] + sib_sums[index]
         squares = jnp.sum(jnp.where(lane == RANK, total, 0.0), axis=1, keepdims=True)
         scale = lax.rsqrt(squares / (WIDTH * 32) + 1e-05)
@@ -370,44 +334,45 @@
                 part = lax.rem(index, per_micro)
                 pltpu.make_async_copy(next_h.at[index], finished.at[part], fr.at[part]).start()
 
+    def retire(index):
+        for phase in range(PHASES):
+            for copy in phase_copies(index, phase):
+                copy.wait_send()
+        for copy in swaps(index):
+            copy.wait_send()
+
     pltpu.make_async_copy(narrow_t, narrow_t, once.at[7]).wait()
-    pltpu.make_async_copy(widen_t, widen_t, once.at[5]).wait()
-    pltpu.make_async_copy(w_own, w_own, once.at[1]).wait()
-    pltpu.make_async_copy(w_sib, w_sib, once.at[3]).wait()
-    pltpu.make_async_copy(w_sib, w_sib, once.at[2]).wait()
-    pltpu.make_async_copy(narrow_t.at[pl.ds(0, 31)], narrow_t.at[pl.ds(0, 31)], once.at[6]).wait()
-    pltpu.make_async_copy(widen_t.at[pl.ds(0, 31)], widen_t.at[pl.ds(0, 31)], once.at[4]).wait()
-
-    @pl.loop(0, chunks + 2)
+
+    @pl.loop(0, chunks + RETIRE)
     def _(tick):
+        @pl.when(tick < chunks)
+        def _():
+            prepare(tick)
+
         @pl.when((tick >= 1) & (tick <= chunks))
         def _():
-            finish_step(tick - 1, 2)
-            start_step(tick - 1, 3)
-
-        @pl.when(tick < chunks)
-        def _():
-            prepare(tick)
-
-        @pl.when(tick >= 2)
-        def _():
-            finish_step(tick - 2, 3)
+            finish_phase(tick - 1, 0)
+            start_phase(tick - 1, 1)
+
+        @pl.when(tick == 2)
+        def _():
+            pltpu.make_async_copy(w_own, w_own, once.at[1]).wait()
+            pltpu.make_async_copy(w_sib, w_sib, once.at[3]).wait()
+            pltpu.make_async_copy(w_sib, w_sib, once.at[2]).wait()
+            pltpu.make_async_copy(narrow_t.at[pl.ds(0, 31)], narrow_t.at[pl.ds(0, 31)], once.at[6]).wait()
+            pltpu.make_async_copy(widen_t, widen_t, once.at[5]).wait()
+            pltpu.make_async_copy(widen_t.at[pl.ds(0, 31)], widen_t.at[pl.ds(0, 31)], once.at[4]).wait()
+
+        @pl.when((tick >= 2) & (tick <= chunks + 1))
+        def _():
+            finish_phase(tick - 2, 1)
             multiply_sibling(tick - 2)
-
-        @pl.when(tick < chunks)
-        def _():
-            finish_step(tick, 0)
-            start_step(tick, 1)
-
-        @pl.when(tick >= 2)
-        def _():
             multiply_own(tick - 2)
             combine(tick - 2)
 
-        @pl.when(tick < chunks)
-        def _():
-            finish_step(tick, 1)
-            start_step(tick, 2)
+        @pl.when(tick >= RETIRE)
+        def _():
+            retire(tick - RETIRE)
 
     @pl.when(section > 0)
     def _():
@@ -477,9 +442,9 @@
         out_specs=(vmem, vmem),
         scratch_shapes=[
             pltpu.VMEM((chunks, CHUNK, WIDTH), bf16),
-            pltpu.VMEM((chunks, COLOURS, 16, PIECE, WIDTH), bf16),
-            pltpu.VMEM((chunks, STEPS, CHUNK, LANES), bf16),
-            pltpu.VMEM((chunks, STEPS, CHUNK, LANES), bf16),
+            pltpu.VMEM((chunks, COLOURS, RING, RING, PIECE, WIDTH), bf16),
+            pltpu.VMEM((chunks, PHASES, CHUNK, LANES), bf16),
+            pltpu.VMEM((chunks, PHASES, 3, CHUNK, LANES), bf16),
             pltpu.VMEM((chunks, CHUNK, LANES), f32),
             pltpu.VMEM((chunks, CHUNK, LANES), f32),
             pltpu.VMEM((chunks, CHUNK, LANES), f32),
@@ -489,17 +454,15 @@
             pltpu.VMEM((chunks, CHUNK, WIDTH), bf16),
             pltpu.VMEM((16 * WIDTH, WIDTH), bf16),
             pltpu.VMEM((16 * WIDTH, WIDTH), bf16),
-            pltpu.VMEM((32 * WIDTH, RANK), bf16),
-            pltpu.VMEM((32, 128, LANES), bf16),
-            pltpu.VMEM((32, 128, LANES), bf16),
+            pltpu.VMEM((32, RANK, WIDTH), bf16),
             pltpu.VMEM((32, RANK, WIDTH), bf16),
             pltpu.VMEM((256 // CHUNK, CHUNK, WIDTH), bf16),
             pltpu.VMEM((1, 256), f32),
             pltpu.VMEM((32, 1, 256), f32),
-            dma((4, STEPS, COLOURS)),
-            dma((4, STEPS, COLOURS)),
-            dma((4, STEPS, COLOURS)),
-            dma((4, STEPS, COLOURS)),
+            dma((4, PHASES, COLOURS, 3)),
+            dma((4, PHASES, COLOURS, 3)),
+            dma((4, PHASES, COLOURS, 3)),
+            dma((4, PHASES, COLOURS, 3)),
             dma((4, 2)),
             dma((4, 2)),
             dma((chunks,)),
@@ -517,7 +480,7 @@
         entering_hidden[0],
         section_weight[0],
         section_norm_gain,
-        plugin_narrowing_factors[0, 0],
+        plugin_narrowing_factors[0, 0].T,
         plugin_widening_factors[0, 0],
         reward_head[None, :],
     )

time: 338 us -> 174 us (0.51)
  Pallas kernels: 329 us -> 168 us
    pallas_call x1, Pallas kernels: 329 us -> 168 us  [shards(): pl.pallas_call(functools.partial(kernel, chunks), out_shape=(jax.ShapeDty...]
    unnamed x4 -> x3, local copies, waits for them, and re-layouts: 6.91 us -> 4.13 us
where the time goes in v2:
time: 174 us
  Pallas kernels  168 us (97%)
  local copies, waits for them, and re-layouts  5.35 us (3%)
    pallas_call x1, Pallas kernels, shards(): pl.pallas_call(functools.partial(kernel, chunks), out_shape=(jax.ShapeDty...  168 us
    unnamed x3, local copies, waits for them, and re-layouts  4.13 us

profile of v2, /device:TPU:97, one launch (start us, length us, event | category | flops | bytes accessed | tf_op | source)
XLA Modules:
  0.0 173.6 jit_solution(8504963496329137457)
XLA Ops:
  0.6 1.2 broadcast_in_dim.6.head_ref
  1.9 1.3 copy.10.adapter_ref
  3.2 167.6 %shard_map.95 = (bf16[256,256]{1,0:T(8,128)(2,1)}, f32[1,256]{1,0:T(1,128)}) custom-call(s32[4,2]{1,0:T(4,128)} %copy.10.adapter_ref, s32[1,2]{1,0:T(1,128)} %live_ref.1, bf16[256,256]{1,0:T(8,128)(2,1)} %bitcast.10, bf16[8192,256]{1,0:T(8,128)(2,1)} %bitcast.7, bf16[1,256]{1,0:T(2,128)(2,1)} %gain_ref.1, bf16[64,8192]{1,0:T(8,128)(2,1)} %bitcast.8, ...), custom_call_target="tpu_custom_call" | custom-call | tf_op jit(solution)/shard_map/pallas_call | solution.py:435
  170.8 1.6 copy.13
  172.3 1.2 copy.14

commit v3 on v2

v3 whole, which is shorter than its diff:
```python
import functools

import jax
import jax.numpy as jnp
from jax import lax
from jax.experimental import pallas as pl
from jax.experimental.pallas import tpu as pltpu
from jax.sharding import PartitionSpec as P

MESH = pl.DeviceIdType.MESH
BLOCK = 128
CHUNK = 64
COLOURS = 2
PHASES = 2
PIECE = CHUNK // COLOURS
RING = 4
WIDTH = 256
RANK = 64
LANES = 128
LATE = 3
RETIRE = 4
DEPTH = 5

FAR = ((2, 2), (3, 2), (2, 3), (1, 2), (2, 1), (0, 2), (2, 0), (3, 1), (1, 3), (3, 3), (1, 1), (0, 3), (3, 0), (0, 1), (1, 0))


def flipped(position, mask):
    if mask == 0:
        return position
    if mask == 1:
        return position + 1 - 2 * lax.rem(position, 2)
    if mask == 2:
        return lax.rem(position + 2, 4)
    return 3 - position


def slot_of(colour, rel):
    return (rel // 4, rel % 4) if colour == 0 else (rel % 4, rel // 4)


def pack(value):
    pieces = []
    for colour in range(COLOURS):
        first = colour * PIECE
        pieces.append(
            jnp.concatenate([value[first : first + PIECE // 2], value[first + PIECE // 2 : first + PIECE]], axis=1)
        )
    return jnp.concatenate(pieces, axis=0)


def unpack(value):
    pieces = []
    for colour in range(COLOURS):
        piece = value[colour * PIECE // 2 : (colour + 1) * PIECE // 2]
        pieces += [piece[:, :RANK], piece[:, RANK:]]
    return jnp.concatenate(pieces, axis=0)


def kernel(
    chunks,
    adapter_ref,
    live_ref,
    enter_ref,
    weight_ref,
    gain_ref,
    narrow_ref,
    widen_ref,
    head_ref,
    out_ref,
    score_ref,
    gathered,
    sums_out,
    sums_in,
    running,
    final_sums,
    sib_sums,
    part_out,
    part_in,
    own_part,
    next_h,
    w_own,
    w_sib,
    narrow_t,
    widen_t,
    gain_o,
    gains,
    finished,
    score_part,
    score_all,
    gs,
    gr,
    as_,
    ar_,
    xs,
    xr,
    zs,
    zo,
    zr,
    fs,
    fr,
    once,
):
    section = lax.axis_index("section")
    mp = lax.axis_index("mp")
    core = lax.rem(mp, 2)
    chip = lax.div(mp, 2)
    x = lax.rem(chip, RING)
    y = lax.div(chip, RING)
    other = mp + 1 - 2 * core
    per_micro = 256 // CHUNK

    def mesh_id(where, rank):
        return {"section": where, "mp": rank}

    barrier = pltpu.get_barrier_semaphore()
    for offset in range(1, 32):
        pl.semaphore_signal(
            barrier, inc=1, device_id=mesh_id(section, lax.rem(mp + offset, 32)), device_id_type=MESH
        )
    for offset in range(1, 4):
        pl.semaphore_signal(
            barrier, inc=1, device_id=mesh_id(lax.rem(section + offset, 4), mp), device_id_type=MESH
        )

    def chip_of(rel):
        return flipped(y, rel // 4) * RING + flipped(x, rel % 4)

    for rel in range(16):
        rows = pl.ds(pl.multiple_of((chip_of(rel) * 2 + core) * WIDTH, WIDTH), WIDTH)
        pltpu.make_async_copy(
            weight_ref.at[rows], w_own.at[pl.ds(rel * WIDTH, WIDTH)], once.at[1]
        ).start()

    @pl.when(section == 0)
    def _():
        for part in range(per_micro):
            for colour in range(COLOURS):
                pltpu.make_async_copy(
                    enter_ref.at[pl.ds(part * CHUNK + colour * PIECE, PIECE)],
                    gathered.at[part, colour, 0, 0],
                    zr.at[part, colour],
                ).start()

    pl.semaphore_wait(barrier, 34)

    @pl.when(section > 0)
    def _():
        for part in range(per_micro):
            index = section * per_micro + part
            for colour in range(COLOURS):
                pltpu.make_async_remote_copy(
                    src_ref=enter_ref.at[pl.ds(part * CHUNK + colour * PIECE, PIECE)],
                    dst_ref=gathered.at[index, colour, 0, 0],
                    send_sem=fs.at[part, colour],
                    recv_sem=zr.at[index, colour],
                    device_id=mesh_id(0, mp),
                    device_id_type=MESH,
                ).start()

    def swap_weight(rel):
        rows = pl.ds(pl.multiple_of((chip_of(rel) * 2 + 1 - core) * WIDTH, WIDTH), WIDTH)
        return pltpu.make_async_remote_copy(
            src_ref=weight_ref.at[rows],
            dst_ref=w_sib.at[pl.ds(rel * WIDTH, WIDTH)],
            send_sem=once.at[2],
            recv_sem=once.at[3],
            device_id=mesh_id(section, other),
            device_id_type=MESH,
        )

    def columns(rank):
        return pl.ds(pl.multiple_of(rank * WIDTH, WIDTH), WIDTH)

    def spread(source, table, send, receive):
        for other_core in (0, 1):
            for mask_x, mask_y in FAR + (((0, 0),) if other_core else ()):
                rank = (flipped(y, mask_y) * RING + flipped(x, mask_x)) * 2 + (1 - core if other_core else core)
                pltpu.make_async_remote_copy(
                    src_ref=source.at[:, columns(rank)],
                    dst_ref=table.at[mp],
                    send_sem=once.at[send],
                    recv_sem=once.at[receive],
                    device_id=mesh_id(section, rank),
                    device_id_type=MESH,
                ).start()

    def spread_own(source, table, receive):
        pltpu.make_async_copy(source.at[:, columns(mp)], table.at[mp], once.at[receive]).start()

    def full_wait(table, semaphore):
        pltpu.make_async_copy(table, table, once.at[semaphore]).wait()

    def part_wait(table, semaphore):
        part = table.at[pl.ds(0, 31)]
        pltpu.make_async_copy(part, part, once.at[semaphore]).wait()

    for rel in range(16):
        swap_weight(rel).start()
    spread(narrow_ref, narrow_t, 6, 7)
    spread_own(narrow_ref, narrow_t, 7)
    spread(widen_ref, widen_t, 4, 5)
    spread_own(widen_ref, widen_t, 5)
    gain_o[...] = gain_ref[...].astype(jnp.float32)
    for mask_x, mask_y in FAR:
        pltpu.make_async_remote_copy(
            src_ref=gain_o,
            dst_ref=gains.at[mask_y * RING + mask_x],
            send_sem=once.at[8],
            recv_sem=once.at[9],
            device_id=mesh_id(section, (flipped(y, mask_y) * RING + flipped(x, mask_x)) * 2 + core),
            device_id_type=MESH,
        ).start()
    pltpu.make_async_copy(gain_o, gains.at[0], once.at[9]).start()

    def fold_gains():
        full_wait(w_own, 1)
        full_wait(w_sib, 3)
        full_wait(w_sib, 2)
        full_wait(gains, 9)
        pltpu.make_async_copy(gains.at[pl.ds(0, 15)], gains.at[pl.ds(0, 15)], once.at[8]).wait()

        @pl.loop(0, 16)
        def _(rel):
            rows = pl.ds(pl.multiple_of(rel * WIDTH, WIDTH), WIDTH)
            diagonal = lax.broadcasted_iota(jnp.int32, (WIDTH, WIDTH), 0) == lax.broadcasted_iota(
                jnp.int32, (WIDTH, WIDTH), 1
            )
            factor = jnp.sum(jnp.where(diagonal, gains[rel], 0.0), axis=1, keepdims=True)
            w_own[rows] = (w_own[rows].astype(jnp.float32) * factor).astype(jnp.bfloat16)
            w_sib[rows] = (w_sib[rows].astype(jnp.float32) * factor).astype(jnp.bfloat16)

    fold_gains()

    def adapter_of(index):
        return adapter_ref[lax.div(lax.rem(index, per_micro), BLOCK // CHUNK), lax.div(index, per_micro)]

    def partner_of(colour, phase, mask):
        mask_x, mask_y = (mask, 0) if colour == phase else (0, mask)
        return (flipped(y, mask_y) * RING + flipped(x, mask_x)) * 2 + core

    def colour_rows(colour):
        return pl.ds(colour * (PIECE // 2), PIECE // 2)

    def remote(source, target, send, receive, plane, rank):
        return pltpu.make_async_remote_copy(
            src_ref=source,
            dst_ref=target,
            send_sem=send,
            recv_sem=receive,
            device_id=mesh_id(plane, rank),
            device_id_type=MESH,
        )

    def first_rows(index):
        ring_slot = lax.rem(index, DEPTH)
        return [
            remote(
                gathered.at[index, colour, 0, 0],
                gathered.at[index, colour, 0, mask],
                gs.at[ring_slot, 0, colour, mask - 1],
                gr.at[ring_slot, 0, colour, mask - 1],
                section,
                partner_of(colour, 0, mask),
            )
            for mask in (2, 3, 1)
            for colour in range(COLOURS)
        ]

    def first_sums(index):
        ring_slot = lax.rem(index, DEPTH)
        return [
            remote(
                sums_in.at[index, 0, 0, colour_rows(colour)],
                sums_in.at[index, 0, mask, colour_rows(colour)],
                as_.at[ring_slot, 0, colour, mask - 1],
                ar_.at[ring_slot, 0, colour, mask - 1],
                section,
                partner_of(colour, 0, mask),
            )
            for mask in (2, 3, 1)
            for colour in range(COLOURS)
        ]

    def second_copies(index):
        ring_slot = lax.rem(index, DEPTH)
        copies = []
        for mask in (2, 3, 1):
            for colour in range(COLOURS):
                rank = partner_of(colour, 1, mask)
                rows = colour_rows(colour)
                copies.append(
                    remote(
                        gathered.at[index, colour, 0],
                        gathered.at[index, colour, mask],
                        gs.at[ring_slot, 1, colour, mask - 1],
                        gr.at[ring_slot, 1, colour, mask - 1],
                        section,
                        rank,
                    )
                )
                copies.append(
                    remote(
                        sums_out.at[index, rows],
                        sums_in.at[index, 1, mask, rows],
                        as_.at[ring_slot, 1, colour, mask - 1],
                        ar_.at[ring_slot, 1, colour, mask - 1],
                        section,
                        rank,
                    )
                )
        return copies

    def relay(index):
        for copy in first_rows(index) + first_sums(index):
            copy.wait_recv()
        total = sums_in[index, 0, 0].astype(jnp.float32)
        for mask in (1, 2, 3):
            total = total + sums_in[index, 0, mask].astype(jnp.float32)
        running[index] = total
        sums_out[index] = total.astype(jnp.bfloat16)
        for copy in second_copies(index):
            copy.start()

    def finish_gather(index):
        for copy in second_copies(index):
            copy.wait_recv()
        total = running[index]
        for mask in (1, 2, 3):
            total = total + sums_in[index, 1, mask].astype(jnp.float32)
        rows = left_side(index).astype(jnp.float32)
        squares = jnp.sum(rows * rows, axis=1, keepdims=True)
        final_sums[index] = jnp.concatenate(
            [unpack(total), jnp.broadcast_to(squares, (CHUNK, LANES - RANK))], axis=1
        )

    def inner_products(h, scale_by, maps):
        scaled = (h.astype(jnp.float32) * scale_by).astype(jnp.bfloat16)
        inner = lax.dot_general(scaled, maps, (((1,), (1,)), ((), ())), preferred_element_type=jnp.float32)
        return pack(inner).astype(jnp.bfloat16)

    def own_rows(index):
        return jnp.concatenate([gathered[index, colour, 0, 0] for colour in range(COLOURS)], axis=0)

    def feed(index):
        for colour in range(COLOURS):
            piece = gathered.at[index, colour, 0, 0]
            pltpu.make_async_copy(piece, piece, zr.at[index, colour]).wait()
        for copy in first_rows(index):
            copy.start()
        sums_in[index, 0, 0] = inner_products(own_rows(index), gain_o[...], narrow_t[adapter_of(index)])
        for copy in first_sums(index):
            copy.start()

    def left_side(index):
        return jnp.concatenate(
            [
                jnp.concatenate([gathered[(index, colour) + slot_of(colour, rel)] for colour in range(COLOURS)], axis=0)
                for rel in range(16)
            ],
            axis=1,
        )

    def swaps(index):
        ring_slot = lax.rem(index, DEPTH)
        sums = pltpu.make_async_remote_copy(
            src_ref=final_sums.at[index],
            dst_ref=sib_sums.at[index],
            send_sem=xs.at[ring_slot, 0],
            recv_sem=xr.at[ring_slot, 0],
            device_id=mesh_id(section, other),
            device_id_type=MESH,
        )
        parts = pltpu.make_async_remote_copy(
            src_ref=part_out.at[index],
            dst_ref=part_in.at[index],
            send_sem=xs.at[ring_slot, 1],
            recv_sem=xr.at[ring_slot, 1],
            device_id=mesh_id(section, other),
            device_id_type=MESH,
        )
        return sums, parts

    def multiply_sibling(index):
        sums, parts = swaps(index)
        sums.start()
        part_out[index] = jnp.dot(left_side(index), w_sib[...], preferred_element_type=jnp.float32)
        parts.start()

    def multiply_own(index):
        own_part[...] = jnp.dot(left_side(index), w_own[...], preferred_element_type=jnp.float32)

    def onward(index):
        ring_slot = lax.rem(index, DEPTH)
        return [
            remote(
                next_h.at[index, pl.ds(colour * PIECE, PIECE)],
                gathered.at[index, colour, 0, 0],
                zo.at[ring_slot, colour],
                zr.at[index, colour],
                section + 1,
                mp,
            )
            for colour in range(COLOURS)
        ]

    def homeward(index):
        home = lax.div(index, per_micro)
        part = lax.rem(index, per_micro)
        return pltpu.make_async_remote_copy(
            src_ref=next_h.at[index],
            dst_ref=finished.at[part],
            send_sem=zs.at[index],
            recv_sem=fr.at[part],
            device_id=mesh_id(home, mp),
            device_id_type=MESH,
        )

    def combine(index):
        sums, parts = swaps(index)
        sums.wait_recv()
        total = final_sums[index] + sib_sums[index]
        squares = total[:, RANK : RANK + 1]
        scale = lax.rsqrt(squares / (WIDTH * 32) + 1e-05)
        inner = total[:, :RANK].astype(jnp.bfloat16)
        delta = jnp.dot(inner, widen_t[adapter_of(index)], preferred_element_type=jnp.float32)
        own = own_part[...] + 2.0 * delta
        parts.wait_recv()
        base = own + part_in[index]
        h = own_rows(index).astype(jnp.float32)
        result = (h + scale * base).astype(jnp.bfloat16)
        next_h[index] = result

        @pl.when(section < 3)
        def _():
            for copy in onward(index):
                copy.start()

        @pl.when(section == 3)
        def _():
            @pl.when(index < 3 * per_micro)
            def _():
                homeward(index).start()

            @pl.when(index >= 3 * per_micro)
            def _():
                part = lax.rem(index, per_micro)
                pltpu.make_async_copy(next_h.at[index], finished.at[part], fr.at[part]).start()

    def retire(index):
        for copy in first_rows(index) + first_sums(index) + second_copies(index):
            copy.wait_send()
        for copy in swaps(index):
            copy.wait_send()

        @pl.when(section < 3)
        def _():
            for copy in onward(index):
                copy.wait_send()

    full_wait(narrow_t, 7)

    @pl.loop(0, chunks + RETIRE)
    def _(tick):
        @pl.when(tick < chunks)
        def _():
            feed(tick)

        @pl.when(tick == LATE)
        def _():
            part_wait(narrow_t, 6)
            full_wait(widen_t, 5)
            part_wait(widen_t, 4)

        @pl.when((tick >= LATE) & (tick < chunks + LATE))
        def _():
            finish_gather(tick - LATE)
            multiply_sibling(tick - LATE)

        @pl.when((tick >= 1) & (tick <= chunks))
        def _():
            relay(tick - 1)

        @pl.when((tick >= LATE) & (tick < chunks + LATE))
        def _():
            multiply_own(tick - LATE)
            combine(tick - LATE)

        @pl.when(tick >= RETIRE)
        def _():
            retire(tick - RETIRE)

    @pl.when(section > 0)
    def _():
        for part in range(per_micro):
            for colour in range(COLOURS):
                piece = gathered.at[0, colour, 0, 0]
                pltpu.make_async_copy(piece, piece, fs.at[part, colour]).wait()

    @pl.when(section == 3)
    def _():
        @pl.loop(0, 3 * per_micro)
        def _(index):
            pltpu.make_async_copy(next_h.at[index], next_h.at[index], zs.at[index]).wait()

    for part in range(per_micro):
        pltpu.make_async_copy(finished.at[part], finished.at[part], fr.at[part]).wait()
    hidden = jnp.concatenate([finished[part] for part in range(per_micro)], axis=0)
    out_ref[...] = hidden
    head = jnp.broadcast_to(head_ref[...], (8, WIDTH))
    partial = lax.dot_general(head, hidden, (((1,), (1,)), ((), ())), preferred_element_type=jnp.float32)
    score_part[...] = partial[:1]

    def score_send(offset):
        return pltpu.make_async_remote_copy(
            src_ref=score_part,
            dst_ref=score_all.at[mp],
            send_sem=once.at[14],
            recv_sem=once.at[15],
            device_id=mesh_id(section, lax.rem(mp + offset, 32)),
            device_id_type=MESH,
        )

    @pl.loop(1, 32)
    def _(offset):
        score_send(offset).start()

    pltpu.make_async_copy(score_part, score_all.at[mp], once.at[15]).start()
    pltpu.make_async_copy(score_all, score_all, once.at[15]).wait()
    pltpu.make_async_copy(score_all.at[pl.ds(0, 31)], score_all.at[pl.ds(0, 31)], once.at[14]).wait()
    raw = jnp.sum(score_all[...], axis=0)
    place = lax.broadcasted_iota(jnp.int32, (1, 2 * BLOCK), 1)
    limit = jnp.where(place < BLOCK, live_ref[0, 0], live_ref[0, 1])
    score_ref[...] = jnp.where(lax.rem(place, BLOCK) < limit, raw, 0.0)


def shards(
    entering_hidden,
    section_weight,
    section_norm_gain,
    plugin_narrowing_factors,
    plugin_widening_factors,
    reward_head,
    adapter_of_block,
    live_block_rows,
):
    chunks = 1024 // CHUNK
    bf16, f32 = jnp.bfloat16, jnp.float32
    vmem = pl.BlockSpec(memory_space=pltpu.VMEM)
    smem = pl.BlockSpec(memory_space=pltpu.SMEM)
    anywhere = pl.BlockSpec(memory_space=pl.ANY)
    dma = pltpu.SemaphoreType.DMA
    hidden, scores = pl.pallas_call(
        functools.partial(kernel, chunks),
        out_shape=(
            jax.ShapeDtypeStruct((256, WIDTH), bf16),
            jax.ShapeDtypeStruct((1, 256), f32),
        ),
        in_specs=[smem, smem, anywhere, anywhere, vmem, anywhere, anywhere, vmem],
        out_specs=(vmem, vmem),
        scratch_shapes=[
            pltpu.VMEM((chunks, COLOURS, RING, RING, PIECE, WIDTH), bf16),
            pltpu.VMEM((chunks, CHUNK // 2, LANES), bf16),
            pltpu.VMEM((chunks, PHASES, RING, CHUNK // 2, LANES), bf16),
            pltpu.VMEM((chunks, CHUNK // 2, LANES), f32),
            pltpu.VMEM((chunks, CHUNK, LANES), f32),
            pltpu.VMEM((chunks, CHUNK, LANES), f32),
            pltpu.VMEM((chunks, CHUNK, WIDTH), f32),
            pltpu.VMEM((chunks, CHUNK, WIDTH), f32),
            pltpu.VMEM((CHUNK, WIDTH), f32),
            pltpu.VMEM((chunks, CHUNK, WIDTH), bf16),
            pltpu.VMEM((16 * WIDTH, WIDTH), bf16),
            pltpu.VMEM((16 * WIDTH, WIDTH), bf16),
            pltpu.VMEM((32, RANK, WIDTH), bf16),
            pltpu.VMEM((32, RANK, WIDTH), bf16),
            pltpu.VMEM((1, WIDTH), f32),
            pltpu.VMEM((16, 1, WIDTH), f32),
            pltpu.VMEM((256 // CHUNK, CHUNK, WIDTH), bf16),
            pltpu.VMEM((1, 256), f32),
            pltpu.VMEM((32, 1, 256), f32),
            dma((DEPTH, PHASES, COLOURS, 3)),
            dma((DEPTH, PHASES, COLOURS, 3)),
            dma((DEPTH, PHASES, COLOURS, 3)),
            dma((DEPTH, PHASES, COLOURS, 3)),
            dma((DEPTH, 2)),
            dma((DEPTH, 2)),
            dma((chunks,)),
            dma((DEPTH, COLOURS)),
            dma((chunks, COLOURS)),
            dma((4, COLOURS)),
            dma((4,)),
            dma((16,)),
        ],
        compiler_params=pltpu.CompilerParams(
            collective_id=0, has_side_effects=True, vmem_limit_bytes=60 * 1024 * 1024
        ),
    )(
        adapter_of_block.T,
        live_block_rows,
        entering_hidden[0],
        section_weight[0],
        section_norm_gain,
        plugin_narrowing_factors[0, 0].T,
        plugin_widening_factors[0, 0],
        reward_head[None, :],
    )
    return hidden[None], scores


def solution(mesh):
    placed = (
        P("section", None, "mp"),
        P("section", None, "mp"),
        P("section", "mp"),
        P("section", "mp", None, None),
        P("section", "mp", None, None),
        P("mp"),
        P(),
        P("section", None),
    )
    return jax.shard_map(
        shards,
        mesh=mesh,
        in_specs=placed,
        out_specs=(P("section", None, "mp"), P("section", None)),
        check_vma=False,
    )
```

time: 174 us -> 163 us (0.937)
  Pallas kernels: 168 us -> 158 us
    pallas_call x1, Pallas kernels: 168 us -> 158 us  [shards(): pl.pallas_call(functools.partial(kernel, chunks), out_shape=(jax.ShapeDty...]
    unnamed x3 -> x2, local copies, waits for them, and re-layouts: 4.13 us -> 2.8 us
where the time goes in v3:
time: 163 us; the launch traced here: 162 us
  Pallas kernels  158 us (97%)
  local copies, waits for them, and re-layouts  4.02 us (2%)
    pallas_call x1, Pallas kernels, shards(): pl.pallas_call(functools.partial(kernel, chunks), out_shape=(jax.ShapeDty...  158 us

profile of v3, /device:TPU:97, one launch (start us, length us, event | category | flops | bytes accessed | tf_op | source)
XLA Modules:
  0.0 162.5 jit_solution(3720440389017427389)
XLA Ops:
  0.6 1.2 broadcast_in_dim.6.head_ref
  1.9 157.8 %shard_map.95 = (bf16[256,256]{1,0:T(8,128)(2,1)}, f32[1,256]{1,0:T(1,128)}) custom-call(s32[2,4]{1,0:T(2,128)} %bitcast.13, s32[1,2]{1,0:T(1,128)} %live_ref.1, bf16[256,256]{1,0:T(8,128)(2,1)} %bitcast.12, bf16[8192,256]{1,0:T(8,128)(2,1)} %bitcast.8, bf16[1,256]{1,0:T(2,128)(2,1)} %gain_ref.1, bf16[64,8192]{1,0:T(8,128)(2,1)} %bitcast.9, ...), custom_call_target="tpu_custom_call" | custom-call | tf_op jit(solution)/shard_map/pallas_call | solution.py:552
  159.7 1.6 copy.12
  161.2 1.2 copy.13

commit v4 on v3

--- a/solution.py
+++ b/solution.py
@@ -17,9 +17,9 @@
 WIDTH = 256
 RANK = 64
 LANES = 128
-LATE = 3
-RETIRE = 4
-DEPTH = 5
+LATE = 4
+RETIRE = 5
+DEPTH = 6
 
 FAR = ((2, 2), (3, 2), (2, 3), (1, 2), (2, 1), (0, 2), (2, 0), (3, 1), (1, 3), (3, 3), (1, 1), (0, 3), (3, 0), (0, 1), (1, 0))
 
@@ -80,6 +80,8 @@
     next_h,
     w_own,
     w_sib,
+    narrow_s,
+    widen_s,
     narrow_t,
     widen_t,
     gain_o,
@@ -91,6 +93,8 @@
     gr,
     as_,
     ar_,
+    ts,
+    tr,
     xs,
     xr,
     zs,
@@ -131,6 +135,14 @@
             weight_ref.at[rows], w_own.at[pl.ds(rel * WIDTH, WIDTH)], once.at[1]
         ).start()
 
+    def columns(rank):
+        return pl.ds(pl.multiple_of(rank * WIDTH, WIDTH), WIDTH)
+
+    for rank in range(32):
+        pltpu.make_async_copy(narrow_ref.at[:, columns(rank)], narrow_s.at[rank], once.at[0]).start()
+    for rank in range(32):
+        pltpu.make_async_copy(widen_ref.at[:, columns(rank)], widen_s.at[rank], once.at[10]).start()
+
     @pl.when(section == 0)
     def _():
         for part in range(per_micro):
@@ -168,15 +180,12 @@
             device_id_type=MESH,
         )
 
-    def columns(rank):
-        return pl.ds(pl.multiple_of(rank * WIDTH, WIDTH), WIDTH)
-
     def spread(source, table, send, receive):
         for other_core in (0, 1):
             for mask_x, mask_y in FAR + (((0, 0),) if other_core else ()):
                 rank = (flipped(y, mask_y) * RING + flipped(x, mask_x)) * 2 + (1 - core if other_core else core)
                 pltpu.make_async_remote_copy(
-                    src_ref=source.at[:, columns(rank)],
+                    src_ref=source.at[rank],
                     dst_ref=table.at[mp],
                     send_sem=once.at[send],
                     recv_sem=once.at[receive],
@@ -185,7 +194,7 @@
                 ).start()
 
     def spread_own(source, table, receive):
-        pltpu.make_async_copy(source.at[:, columns(mp)], table.at[mp], once.at[receive]).start()
+        pltpu.make_async_copy(source.at[mp], table.at[mp], once.at[receive]).start()
 
     def full_wait(table, semaphore):
         pltpu.make_async_copy(table, table, once.at[semaphore]).wait()
@@ -194,12 +203,14 @@
         part = table.at[pl.ds(0, 31)]
         pltpu.make_async_copy(part, part, once.at[semaphore]).wait()
 
+    full_wait(narrow_s, 0)
+    spread(narrow_s, narrow_t, 6, 7)
+    spread_own(narrow_s, narrow_t, 7)
+    full_wait(widen_s, 10)
+    spread(widen_s, widen_t, 4, 5)
+    spread_own(widen_s, widen_t, 5)
     for rel in range(16):
         swap_weight(rel).start()
-    spread(narrow_ref, narrow_t, 6, 7)
-    spread_own(narrow_ref, narrow_t, 7)
-    spread(widen_ref, widen_t, 4, 5)
-    spread_own(widen_ref, widen_t, 5)
     gain_o[...] = gain_ref[...].astype(jnp.float32)
     for mask_x, mask_y in FAR:
         pltpu.make_async_remote_copy(
@@ -281,48 +292,74 @@
             for colour in range(COLOURS)
         ]
 
-    def second_copies(index):
+    def second_rows(index):
         ring_slot = lax.rem(index, DEPTH)
-        copies = []
-        for mask in (2, 3, 1):
-            for colour in range(COLOURS):
-                rank = partner_of(colour, 1, mask)
-                rows = colour_rows(colour)
-                copies.append(
-                    remote(
-                        gathered.at[index, colour, 0],
-                        gathered.at[index, colour, mask],
-                        gs.at[ring_slot, 1, colour, mask - 1],
-                        gr.at[ring_slot, 1, colour, mask - 1],
-                        section,
-                        rank,
-                    )
-                )
-                copies.append(
-                    remote(
-                        sums_out.at[index, rows],
-                        sums_in.at[index, 1, mask, rows],
-                        as_.at[ring_slot, 1, colour, mask - 1],
-                        ar_.at[ring_slot, 1, colour, mask - 1],
-                        section,
-                        rank,
-                    )
-                )
-        return copies
+        return [
+            remote(
+                gathered.at[index, colour, 0],
+                gathered.at[index, colour, mask],
+                gs.at[ring_slot, 1, colour, mask - 1],
+                gr.at[ring_slot, 1, colour, mask - 1],
+                section,
+                partner_of(colour, 1, mask),
+            )
+            for mask in (3, 1)
+            for colour in range(COLOURS)
+        ]
+
+    def third_rows(index):
+        ring_slot = lax.rem(index, DEPTH)
+        return [
+            remote(
+                gathered.at[index, colour, 4 - mask, pl.ds(half, 2)],
+                gathered.at[index, colour, 2, pl.ds(half, 2)],
+                ts.at[ring_slot, colour, half // 2],
+                tr.at[ring_slot, colour, half // 2],
+                section,
+                partner_of(colour, 1, mask),
+            )
+            for mask, half in ((1, 0), (3, 2))
+            for colour in range(COLOURS)
+        ]
+
+    def second_sums(index):
+        ring_slot = lax.rem(index, DEPTH)
+        return [
+            remote(
+                sums_out.at[index, colour_rows(colour)],
+                sums_in.at[index, 1, mask, colour_rows(colour)],
+                as_.at[ring_slot, 1, colour, mask - 1],
+                ar_.at[ring_slot, 1, colour, mask - 1],
+                section,
+                partner_of(colour, 1, mask),
+            )
+            for mask in (2, 3, 1)
+            for colour in range(COLOURS)
+        ]
+
+    def forward(index):
+        for copy in second_rows(index):
+            copy.wait_recv()
+        for copy in third_rows(index):
+            copy.start()
 
     def relay(index):
-        for copy in first_rows(index) + first_sums(index):
+        for copy in first_rows(index):
+            copy.wait_recv()
+        for copy in second_rows(index):
+            copy.start()
+        for copy in first_sums(index):
             copy.wait_recv()
         total = sums_in[index, 0, 0].astype(jnp.float32)
         for mask in (1, 2, 3):
             total = total + sums_in[index, 0, mask].astype(jnp.float32)
         running[index] = total
         sums_out[index] = total.astype(jnp.bfloat16)
-        for copy in second_copies(index):
+        for copy in second_sums(index):
             copy.start()
 
     def finish_gather(index):
-        for copy in second_copies(index):
+        for copy in second_sums(index) + third_rows(index):
             copy.wait_recv()
         total = running[index]
         for mask in (1, 2, 3):
@@ -447,7 +484,7 @@
                 pltpu.make_async_copy(next_h.at[index], finished.at[part], fr.at[part]).start()
 
     def retire(index):
-        for copy in first_rows(index) + first_sums(index) + second_copies(index):
+        for copy in first_rows(index) + first_sums(index) + second_rows(index) + second_sums(index) + third_rows(index):
             copy.wait_send()
         for copy in swaps(index):
             copy.wait_send()
@@ -484,6 +521,10 @@
         def _():
             multiply_own(tick - LATE)
             combine(tick - LATE)
+
+        @pl.when((tick >= 2) & (tick <= chunks + 1))
+        def _():
+            forward(tick - 2)
 
         @pl.when(tick >= RETIRE)
         def _():
@@ -506,7 +547,7 @@
         pltpu.make_async_copy(finished.at[part], finished.at[part], fr.at[part]).wait()
     hidden = jnp.concatenate([finished[part] for part in range(per_micro)], axis=0)
     out_ref[...] = hidden
-    head = jnp.broadcast_to(head_ref[...], (8, WIDTH))
+    head = jnp.broadcast_to(head_ref[...].reshape(1, WIDTH), (8, WIDTH))
     partial = lax.dot_general(head, hidden, (((1,), (1,)), ((), ())), preferred_element_type=jnp.float32)
     score_part[...] = partial[:1]
 
@@ -572,6 +613,8 @@
             pltpu.VMEM((16 * WIDTH, WIDTH), bf16),
             pltpu.VMEM((32, RANK, WIDTH), bf16),
             pltpu.VMEM((32, RANK, WIDTH), bf16),
+            pltpu.VMEM((32, RANK, WIDTH), bf16),
+            pltpu.VMEM((32, RANK, WIDTH), bf16),
             pltpu.VMEM((1, WIDTH), f32),
             pltpu.VMEM((16, 1, WIDTH), f32),
             pltpu.VMEM((256 // CHUNK, CHUNK, WIDTH), bf16),
@@ -581,6 +624,8 @@
             dma((DEPTH, PHASES, COLOURS, 3)),
             dma((DEPTH, PHASES, COLOURS, 3)),
             dma((DEPTH, PHASES, COLOURS, 3)),
+            dma((DEPTH, COLOURS, 2)),
+            dma((DEPTH, COLOURS, 2)),
             dma((DEPTH, 2)),
             dma((DEPTH, 2)),
             dma((chunks,)),
@@ -601,7 +646,7 @@
         section_norm_gain,
         plugin_narrowing_factors[0, 0].T,
         plugin_widening_factors[0, 0],
-        reward_head[None, :],
+        reward_head,
     )
     return hidden[None], scores
 

time: 163 us -> 157 us (0.963)
  Pallas kernels: 158 us -> 154 us
    pallas_call x1, Pallas kernels: 158 us -> 154 us  [shards(): pl.pallas_call(functools.partial(kernel, chunks), out_shape=(jax.ShapeDty...]
where the time goes in v4:
time: 157 us
  Pallas kernels  154 us (98%)
  local copies, waits for them, and re-layouts  2.8 us (2%)
    pallas_call x1, Pallas kernels, shards(): pl.pallas_call(functools.partial(kernel, chunks), out_shape=(jax.ShapeDty...  154 us

profile of v4, /device:TPU:97, one launch (start us, length us, event | category | flops | bytes accessed | tf_op | source)
XLA Modules:
  0.0 157.2 jit_solution(4364707881617673319)
XLA Ops:
  0.6 153.8 %shard_map.95 = (bf16[256,256]{1,0:T(8,128)(2,1)}, f32[1,256]{1,0:T(1,128)}) custom-call(s32[2,4]{1,0:T(2,128)} %bitcast.13, s32[1,2]{1,0:T(1,128)} %live_ref.1, bf16[256,256]{1,0:T(8,128)(2,1)} %bitcast.11, bf16[8192,256]{1,0:T(8,128)(2,1)} %bitcast.8, bf16[1,256]{1,0:T(2,128)(2,1)} %gain_ref.1, bf16[64,8192]{1,0:T(8,128)(2,1)} %bitcast.9, ...), custom_call_target="tpu_custom_call" | custom-call | tf_op jit(solution)/shard_map/pallas_call | solution.py:593
  154.4 1.6 copy.12
  156.0 1.2 copy.13

commit v5 on v4

--- a/solution.py
+++ b/solution.py
@@ -82,6 +82,7 @@
     w_sib,
     narrow_s,
     widen_s,
+    relay_s,
     narrow_t,
     widen_t,
     gain_o,
@@ -138,10 +139,13 @@
     def columns(rank):
         return pl.ds(pl.multiple_of(rank * WIDTH, WIDTH), WIDTH)
 
+    def stage(rank):
+        return lax.rem(rank, 2) * 16 + lax.div(rank, 2)
+
     for rank in range(32):
-        pltpu.make_async_copy(narrow_ref.at[:, columns(rank)], narrow_s.at[rank], once.at[0]).start()
-    for rank in range(32):
-        pltpu.make_async_copy(widen_ref.at[:, columns(rank)], widen_s.at[rank], once.at[10]).start()
+        slot = rank % 2 * 16 + rank // 2
+        pltpu.make_async_copy(narrow_ref.at[:, columns(rank)], narrow_s.at[slot], once.at[0]).start()
+        pltpu.make_async_copy(widen_ref.at[:, columns(rank)], widen_s.at[slot], once.at[10]).start()
 
     @pl.when(section == 0)
     def _():
@@ -185,7 +189,7 @@
             for mask_x, mask_y in FAR + (((0, 0),) if other_core else ()):
                 rank = (flipped(y, mask_y) * RING + flipped(x, mask_x)) * 2 + (1 - core if other_core else core)
                 pltpu.make_async_remote_copy(
-                    src_ref=source.at[rank],
+                    src_ref=source.at[stage(rank)],
                     dst_ref=table.at[mp],
                     send_sem=once.at[send],
                     recv_sem=once.at[receive],
@@ -194,7 +198,7 @@
                 ).start()
 
     def spread_own(source, table, receive):
-        pltpu.make_async_copy(source.at[mp], table.at[mp], once.at[receive]).start()
+        pltpu.make_async_copy(source.at[stage(mp)], table.at[mp], once.at[receive]).start()
 
     def full_wait(table, semaphore):
         pltpu.make_async_copy(table, table, once.at[semaphore]).wait()
@@ -203,12 +207,27 @@
         part = table.at[pl.ds(0, 31)]
         pltpu.make_async_copy(part, part, once.at[semaphore]).wait()
 
+    full_wait(widen_s, 10)
+
+    def aside(half):
+        return pltpu.make_async_remote_copy(
+            src_ref=widen_s.at[pl.ds(half * 16, 16)],
+            dst_ref=relay_s,
+            send_sem=once.at[16 + half],
+            recv_sem=once.at[18],
+            device_id=mesh_id(2 * half + 1, mp),
+            device_id_type=MESH,
+        )
+
+    @pl.when(section == 0)
+    def _():
+        for half in (0, 1):
+            aside(half).start()
+
     full_wait(narrow_s, 0)
     spread(narrow_s, narrow_t, 6, 7)
     spread_own(narrow_s, narrow_t, 7)
-    full_wait(widen_s, 10)
-    spread(widen_s, widen_t, 4, 5)
-    spread_own(widen_s, widen_t, 5)
+
     for rel in range(16):
         swap_weight(rel).start()
     gain_o[...] = gain_ref[...].astype(jnp.float32)
@@ -241,6 +260,25 @@
             w_sib[rows] = (w_sib[rows].astype(jnp.float32) * factor).astype(jnp.bfloat16)
 
     fold_gains()
+
+    @pl.when(lax.rem(section, 2) == 1)
+    def _():
+        full_wait(relay_s, 18)
+        for mask_x, mask_y in FAR + ((0, 0),):
+            target = flipped(y, mask_y) * RING + flipped(x, mask_x)
+            pltpu.make_async_remote_copy(
+                src_ref=relay_s.at[target],
+                dst_ref=widen_t.at[mp],
+                send_sem=once.at[19],
+                recv_sem=once.at[5],
+                device_id=mesh_id(0, target * 2 + lax.div(section, 2)),
+                device_id_type=MESH,
+            ).start()
+
+    @pl.when(section > 0)
+    def _():
+        spread(widen_s, widen_t, 4, 5)
+        spread_own(widen_s, widen_t, 5)
 
     def adapter_of(index):
         return adapter_ref[lax.div(lax.rem(index, per_micro), BLOCK // CHUNK), lax.div(index, per_micro)]
@@ -506,7 +544,19 @@
         def _():
             part_wait(narrow_t, 6)
             full_wait(widen_t, 5)
-            part_wait(widen_t, 4)
+
+            @pl.when(section > 0)
+            def _():
+                part_wait(widen_t, 4)
+
+            @pl.when(lax.rem(section, 2) == 1)
+            def _():
+                full_wait(relay_s, 19)
+
+            @pl.when(section == 0)
+            def _():
+                for half in (0, 1):
+                    aside(half).wait_send()
 
         @pl.when((tick >= LATE) & (tick < chunks + LATE))
         def _():
@@ -613,6 +663,7 @@
             pltpu.VMEM((16 * WIDTH, WIDTH), bf16),
             pltpu.VMEM((32, RANK, WIDTH), bf16),
             pltpu.VMEM((32, RANK, WIDTH), bf16),
+            pltpu.VMEM((16, RANK, WIDTH), bf16),
             pltpu.VMEM((32, RANK, WIDTH), bf16),
             pltpu.VMEM((32, RANK, WIDTH), bf16),
             pltpu.VMEM((1, WIDTH), f32),
@@ -633,7 +684,7 @@
             dma((chunks, COLOURS)),
             dma((4, COLOURS)),
             dma((4,)),
-            dma((16,)),
+            dma((20,)),
         ],
         compiler_params=pltpu.CompilerParams(
             collective_id=0, has_side_effects=True, vmem_limit_bytes=60 * 1024 * 1024

time: 157 us -> 154 us (0.981)
  Pallas kernels: 154 us -> 151 us
    pallas_call x1, Pallas kernels: 154 us -> 151 us  [shards(): pl.pallas_call(functools.partial(kernel, chunks), out_shape=(jax.ShapeDty...]
where the time goes in v5:
time: 154 us
  Pallas kernels  151 us (98%)
  local copies, waits for them, and re-layouts  2.8 us (2%)
    pallas_call x1, Pallas kernels, shards(): pl.pallas_call(functools.partial(kernel, chunks), out_shape=(jax.ShapeDty...  151 us

profile of v5, /device:TPU:97, one launch (start us, length us, event | category | flops | bytes accessed | tf_op | source)
XLA Modules:
  0.0 154.0 jit_solution(10035632739985087580)
XLA Ops:
  0.6 150.5 %shard_map.95 = (bf16[256,256]{1,0:T(8,128)(2,1)}, f32[1,256]{1,0:T(1,128)}) custom-call(s32[2,4]{1,0:T(2,128)} %bitcast.13, s32[1,2]{1,0:T(1,128)} %live_ref.1, bf16[256,256]{1,0:T(8,128)(2,1)} %bitcast.11, bf16[8192,256]{1,0:T(8,128)(2,1)} %bitcast.8, bf16[1,256]{1,0:T(2,128)(2,1)} %gain_ref.1, bf16[64,8192]{1,0:T(8,128)(2,1)} %bitcast.9, ...), custom_call_target="tpu_custom_call" | custom-call | tf_op jit(solution)/shard_map/pallas_call | solution.py:643
  151.2 1.6 %copy.12 = bf16[1,256,256]{2,1,0:T(8,128)(2,1)} copy(bf16[1,256,256]{2,1,0:T(8,128)(2,1)} %bitcast.12) | data formatting | bytes 262144
  152.7 1.2 copy.13

commit v6 on v5

--- a/solution.py
+++ b/solution.py
@@ -18,6 +18,7 @@
 RANK = 64
 LANES = 128
 LATE = 4
+EARLY = 2
 RETIRE = 5
 DEPTH = 6
 
@@ -118,10 +119,14 @@
         return {"section": where, "mp": rank}
 
     barrier = pltpu.get_barrier_semaphore()
-    for offset in range(1, 32):
-        pl.semaphore_signal(
-            barrier, inc=1, device_id=mesh_id(section, lax.rem(mp + offset, 32)), device_id_type=MESH
-        )
+    plane_ranks = [
+        (flipped(y, mask_y) * RING + flipped(x, mask_x)) * 2 + (1 - core if flip else core)
+        for mask_x, mask_y in FAR + ((0, 0),)
+        for flip in (0, 1)
+        if flip or mask_x or mask_y
+    ]
+    for rank in plane_ranks:
+        pl.semaphore_signal(barrier, inc=1, device_id=mesh_id(section, rank), device_id_type=MESH)
     for offset in range(1, 4):
         pl.semaphore_signal(
             barrier, inc=1, device_id=mesh_id(lax.rem(section + offset, 4), mp), device_id_type=MESH
@@ -223,65 +228,6 @@
     def _():
         for half in (0, 1):
             aside(half).start()
-
-    full_wait(narrow_s, 0)
-    spread(narrow_s, narrow_t, 6, 7)
-    spread_own(narrow_s, narrow_t, 7)
-
-    for rel in range(16):
-        swap_weight(rel).start()
-    gain_o[...] = gain_ref[...].astype(jnp.float32)
-    for mask_x, mask_y in FAR:
-        pltpu.make_async_remote_copy(
-            src_ref=gain_o,
-            dst_ref=gains.at[mask_y * RING + mask_x],
-            send_sem=once.at[8],
-            recv_sem=once.at[9],
-            device_id=mesh_id(section, (flipped(y, mask_y) * RING + flipped(x, mask_x)) * 2 + core),
-            device_id_type=MESH,
-        ).start()
-    pltpu.make_async_copy(gain_o, gains.at[0], once.at[9]).start()
-
-    def fold_gains():
-        full_wait(w_own, 1)
-        full_wait(w_sib, 3)
-        full_wait(w_sib, 2)
-        full_wait(gains, 9)
-        pltpu.make_async_copy(gains.at[pl.ds(0, 15)], gains.at[pl.ds(0, 15)], once.at[8]).wait()
-
-        @pl.loop(0, 16)
-        def _(rel):
-            rows = pl.ds(pl.multiple_of(rel * WIDTH, WIDTH), WIDTH)
-            diagonal = lax.broadcasted_iota(jnp.int32, (WIDTH, WIDTH), 0) == lax.broadcasted_iota(
-                jnp.int32, (WIDTH, WIDTH), 1
-            )
-            factor = jnp.sum(jnp.where(diagonal, gains[rel], 0.0), axis=1, keepdims=True)
-            w_own[rows] = (w_own[rows].astype(jnp.float32) * factor).astype(jnp.bfloat16)
-            w_sib[rows] = (w_sib[rows].astype(jnp.float32) * factor).astype(jnp.bfloat16)
-
-    fold_gains()
-
-    @pl.when(lax.rem(section, 2) == 1)
-    def _():
-        full_wait(relay_s, 18)
-        for mask_x, mask_y in FAR + ((0, 0),):
-            target = flipped(y, mask_y) * RING + flipped(x, mask_x)
-            pltpu.make_async_remote_copy(
-                src_ref=relay_s.at[target],
-                dst_ref=widen_t.at[mp],
-                send_sem=once.at[19],
-                recv_sem=once.at[5],
-                device_id=mesh_id(0, target * 2 + lax.div(section, 2)),
-                device_id_type=MESH,
-            ).start()
-
-    @pl.when(section > 0)
-    def _():
-        spread(widen_s, widen_t, 4, 5)
-        spread_own(widen_s, widen_t, 5)
-
-    def adapter_of(index):
-        return adapter_ref[lax.div(lax.rem(index, per_micro), BLOCK // CHUNK), lax.div(index, per_micro)]
 
     def partner_of(colour, phase, mask):
         mask_x, mask_y = (mask, 0) if colour == phase else (0, mask)
@@ -315,6 +261,78 @@
             for colour in range(COLOURS)
         ]
 
+    def feed_rows(index):
+        leaving = first_rows(index)
+        for colour in range(COLOURS):
+            piece = gathered.at[index, colour, 0, 0]
+            pltpu.make_async_copy(piece, piece, zr.at[index, colour]).wait()
+            for copy in leaving[colour::COLOURS]:
+                copy.start()
+
+    @pl.when(section == 0)
+    def _():
+        for index in range(EARLY):
+            feed_rows(index)
+
+    full_wait(narrow_s, 0)
+    spread(narrow_s, narrow_t, 6, 7)
+    spread_own(narrow_s, narrow_t, 7)
+
+    for rel in range(16):
+        swap_weight(rel).start()
+    gain_o[...] = gain_ref[...].astype(jnp.float32)
+    for mask_x, mask_y in FAR:
+        pltpu.make_async_remote_copy(
+            src_ref=gain_o,
+            dst_ref=gains.at[mask_y * RING + mask_x],
+            send_sem=once.at[8],
+            recv_sem=once.at[9],
+            device_id=mesh_id(section, (flipped(y, mask_y) * RING + flipped(x, mask_x)) * 2 + core),
+            device_id_type=MESH,
+        ).start()
+    pltpu.make_async_copy(gain_o, gains.at[0], once.at[9]).start()
+
+    def fold_gains():
+        full_wait(w_own, 1)
+        full_wait(w_sib, 3)
+        full_wait(w_sib, 2)
+        full_wait(gains, 9)
+        pltpu.make_async_copy(gains.at[pl.ds(0, 15)], gains.at[pl.ds(0, 15)], once.at[8]).wait()
+
+        @pl.loop(0, 16)
+        def _(rel):
+            rows = pl.ds(pl.multiple_of(rel * WIDTH, WIDTH), WIDTH)
+            diagonal = lax.broadcasted_iota(jnp.int32, (WIDTH, WIDTH), 0) == lax.broadcasted_iota(
+                jnp.int32, (WIDTH, WIDTH), 1
+            )
+            factor = jnp.sum(jnp.where(diagonal, gains[rel], 0.0), axis=1, keepdims=True)
+            w_own[rows] = (w_own[rows].astype(jnp.float32) * factor).astype(jnp.bfloat16)
+            w_sib[rows] = (w_sib[rows].astype(jnp.float32) * factor).astype(jnp.bfloat16)
+
+    fold_gains()
+
+    @pl.when(lax.rem(section, 2) == 1)
+    def _():
+        full_wait(relay_s, 18)
+        for mask_x, mask_y in FAR + ((0, 0),):
+            target = flipped(y, mask_y) * RING + flipped(x, mask_x)
+            pltpu.make_async_remote_copy(
+                src_ref=relay_s.at[target],
+                dst_ref=widen_t.at[mp],
+                send_sem=once.at[19],
+                recv_sem=once.at[5],
+                device_id=mesh_id(0, target * 2 + lax.div(section, 2)),
+                device_id_type=MESH,
+            ).start()
+
+    @pl.when(section > 0)
+    def _():
+        spread(widen_s, widen_t, 4, 5)
+        spread_own(widen_s, widen_t, 5)
+
+    def adapter_of(index):
+        return adapter_ref[lax.div(lax.rem(index, per_micro), BLOCK // CHUNK), lax.div(index, per_micro)]
+
     def first_sums(index):
         ring_slot = lax.rem(index, DEPTH)
         return [
@@ -376,16 +394,17 @@
         ]
 
     def forward(index):
-        for copy in second_rows(index):
-            copy.wait_recv()
-        for copy in third_rows(index):
-            copy.start()
+        for arriving, leaving in zip(second_rows(index), third_rows(index)):
+            arriving.wait_recv()
+            leaving.start()
 
     def relay(index):
-        for copy in first_rows(index):
-            copy.wait_recv()
-        for copy in second_rows(index):
-            copy.start()
+        arriving, leaving = first_rows(index), second_rows(index)
+        for colour in range(COLOURS):
+            for copy in arriving[colour::COLOURS]:
+                copy.wait_recv()
+            for copy in leaving[colour::COLOURS]:
+                copy.start()
         for copy in first_sums(index):
             copy.wait_recv()
         total = sums_in[index, 0, 0].astype(jnp.float32)
@@ -416,12 +435,7 @@
     def own_rows(index):
         return jnp.concatenate([gathered[index, colour, 0, 0] for colour in range(COLOURS)], axis=0)
 
-    def feed(index):
-        for colour in range(COLOURS):
-            piece = gathered.at[index, colour, 0, 0]
-            pltpu.make_async_copy(piece, piece, zr.at[index, colour]).wait()
-        for copy in first_rows(index):
-            copy.start()
+    def feed_sums(index):
         sums_in[index, 0, 0] = inner_products(own_rows(index), gain_o[...], narrow_t[adapter_of(index)])
         for copy in first_sums(index):
             copy.start()
@@ -538,7 +552,11 @@
     def _(tick):
         @pl.when(tick < chunks)
         def _():
-            feed(tick)
+            @pl.when((section > 0) | (tick >= EARLY))
+            def _():
+                feed_rows(tick)
+
+            feed_sums(tick)
 
         @pl.when(tick == LATE)
         def _():
@@ -601,19 +619,15 @@
     partial = lax.dot_general(head, hidden, (((1,), (1,)), ((), ())), preferred_element_type=jnp.float32)
     score_part[...] = partial[:1]
 
-    def score_send(offset):
-        return pltpu.make_async_remote_copy(
+    for rank in plane_ranks:
+        pltpu.make_async_remote_copy(
             src_ref=score_part,
             dst_ref=score_all.at[mp],
             send_sem=once.at[14],
             recv_sem=once.at[15],
-            device_id=mesh_id(section, lax.rem(mp + offset, 32)),
+            device_id=mesh_id(section, rank),
             device_id_type=MESH,
-        )
-
-    @pl.loop(1, 32)
-    def _(offset):
-        score_send(offset).start()
+        ).start()
 
     pltpu.make_async_copy(score_part, score_all.at[mp], once.at[15]).start()
     pltpu.make_async_copy(score_all, score_all, once.at[15]).wait()

time: 154 us -> 154 us (level)
  no operation moved by 1% of the time
where the time goes in v6:
time: 154 us
  Pallas kernels  150 us (97%)
  local copies, waits for them, and re-layouts  2.8 us (2%)
    pallas_call x1, Pallas kernels, shards(): pl.pallas_call(functools.partial(kernel, chunks), out_shape=(jax.ShapeDty...  150 us

profile of v6, /device:TPU:97, one launch (start us, length us, event | category | flops | bytes accessed | tf_op | source)
XLA Modules:
  0.0 153.6 jit_solution(12185365044196443498)
XLA Ops:
  0.6 150.2 %shard_map.95 = (bf16[256,256]{1,0:T(8,128)(2,1)}, f32[1,256]{1,0:T(1,128)}) custom-call(s32[2,4]{1,0:T(2,128)} %bitcast.13, s32[1,2]{1,0:T(1,128)} %live_ref.1, bf16[256,256]{1,0:T(8,128)(2,1)} %bitcast.11, bf16[8192,256]{1,0:T(8,128)(2,1)} %bitcast.8, bf16[1,256]{1,0:T(2,128)(2,1)} %gain_ref.1, bf16[64,8192]{1,0:T(8,128)(2,1)} %bitcast.9, ...), custom_call_target="tpu_custom_call" | custom-call | tf_op jit(solution)/shard_map/pallas_call | solution.py:657
  150.8 1.6 %copy.12 = bf16[1,256,256]{2,1,0:T(8,128)(2,1)} copy(bf16[1,256,256]{2,1,0:T(8,128)(2,1)} %bitcast.12) | data formatting | bytes 262144
  152.4 1.2 copy.13

commit v7 on v6

--- a/solution.py
+++ b/solution.py
@@ -515,14 +515,15 @@
         own = own_part[...] + 2.0 * delta
         parts.wait_recv()
         base = own + part_in[index]
-        h = own_rows(index).astype(jnp.float32)
-        result = (h + scale * base).astype(jnp.bfloat16)
-        next_h[index] = result
-
-        @pl.when(section < 3)
-        def _():
-            for copy in onward(index):
-                copy.start()
+        leaving = onward(index)
+        for colour in range(COLOURS):
+            rows = slice(colour * PIECE, (colour + 1) * PIECE)
+            h = gathered[index, colour, 0, 0].astype(jnp.float32)
+            next_h[index, rows] = (h + scale[rows] * base[rows]).astype(jnp.bfloat16)
+
+            @pl.when(section < 3)
+            def _(colour=colour):
+                leaving[colour].start()
 
         @pl.when(section == 3)
         def _():

time: 154 us -> 154 us (level)
  no operation moved by 1% of the time
where the time goes in v7:
time: 154 us
  Pallas kernels  150 us (97%)
  local copies, waits for them, and re-layouts  2.8 us (2%)
    pallas_call x1, Pallas kernels, shards(): pl.pallas_call(functools.partial(kernel, chunks), out_shape=(jax.ShapeDty...  150 us

profile of v7, /device:TPU:97, one launch (start us, length us, event | category | flops | bytes accessed | tf_op | source)
XLA Modules:
  0.0 153.5 jit_solution(7945216719588926811)
XLA Ops:
  0.6 150.1 %shard_map.95 = (bf16[256,256]{1,0:T(8,128)(2,1)}, f32[1,256]{1,0:T(1,128)}) custom-call(s32[2,4]{1,0:T(2,128)} %bitcast.13, s32[1,2]{1,0:T(1,128)} %live_ref.1, bf16[256,256]{1,0:T(8,128)(2,1)} %bitcast.11, bf16[8192,256]{1,0:T(8,128)(2,1)} %bitcast.8, bf16[1,256]{1,0:T(2,128)(2,1)} %gain_ref.1, bf16[64,8192]{1,0:T(8,128)(2,1)} %bitcast.9, ...), custom_call_target="tpu_custom_call" | custom-call | tf_op jit(solution)/shard_map/pallas_call | solution.py:658
  150.7 1.6 %copy.12 = bf16[1,256,256]{2,1,0:T(8,128)(2,1)} copy(bf16[1,256,256]{2,1,0:T(8,128)(2,1)} %bitcast.12) | data formatting | bytes 262144
  152.3 1.2 copy.13
